TPU v7x, 32 devices: a whole 2x2x4 slice. The times are simulated.
32 devices in a mesh: dp: 8 (over z, y), sp: 4 (over x, core).
Axes of the slice: x: 2, y: 2, z: 4, core: 2. Of those that a mesh axis runs over, the one named last changes fastest.
Arguments:
- tokens: bfloat16 [32, 512, 768], P('dp', 'sp'), may hold values from -6 to 6
- output_grad: bfloat16 [32, 512, 768], P('dp', 'sp'), may hold values from -6 to 6
- segment_ids: int32 [32, 512], P('dp'), may hold values from 0 to 7, as said below
- lengths: int32 [32, 8], P('dp'), may hold values from 1 to 128, as said below
- owner_slot: int32 [48], replicated, may hold values from 0 to 47, as said below
- slot_weights: float32 [48, 384, 384], P('dp')
- first_moment: float32 [48, 384, 384], P('dp'), may hold values from -224 to 224
- second_moment: float32 [48, 384, 384], P('dp'), may hold values from 819.2 to 13107.2
- left_stats: float32 [48, 384, 384], P('dp'), as said below
- right_stats: float32 [48, 384, 384], P('dp'), as said below
- left_basis: float32 [48, 384, 384], P('dp'), as said below
- right_basis: float32 [48, 384, 384], P('dp'), as said below
- vector_values: float32 [3072], P('dp')
- vector_first: float32 [3072], P('dp'), may hold values from -768 to 768
- vector_second: float32 [3072], P('dp'), may hold values from 8192 to 131072
Outputs:
- block_out: bfloat16 [32, 512, 768], P('dp', 'sp')
- input_grad: float32 [32, 512, 768], P('dp', 'sp')
- moment_one: float32 [48, 384, 384], P('dp')
- moment_two: float32 [48, 384, 384], P('dp')
- left_new: float32 [48, 384, 384], P('dp')
- right_new: float32 [48, 384, 384], P('dp')
- weights_new: float32 [48, 384, 384], P('dp')
- weights_half: bfloat16 [48, 384, 384], P('dp')
- vector_one: float32 [3072], P('dp')
- vector_two: float32 [3072], P('dp')
- vector_new: float32 [3072], P('dp')
Inputs may be any that keep to these rules, and one draw needn't show every extreme that they name: `segment_ids`: token t of a row carries passage p iff the sum of that row's first p lengths is at most t and the sum of its first p + 1 lengths is over t. Each row's lengths sum to 512; one length of every row is exactly 128. distinct; block b lies at place owner_slot[b] % 6 of index owner_slot[b] // 6 of dp; some index holds 6 blocks. `left_stats`: each block symmetric and positive definite. `right_stats`: each block symmetric and positive definite. `left_basis`: each block orthogonal. `right_basis`: each block orthogonal.
All inputs are finite; a program needn't handle non-finite values.
Results may differ from a plain program's by a relative error of at most 0.017.
Values may be sent and summed in bfloat16 or wider, within the bound.
A program may use at most 256 MiB of HBM per device.

v0:
```python
import jax
import jax.numpy as jnp
from jax import lax
from jax.sharding import PartitionSpec as P

D = 768
HD = 64
FF = 3072
BLK = 384
STEP = 4


highest = lax.Precision.HIGHEST
rate_matrix = 0.04
rate_vector = 0.2


def layer_norm(summed, gain, shift):
    centre = jnp.mean(summed, axis=-1, keepdims=True)
    centred = summed - centre
    spread = jnp.mean(centred * centred, axis=-1, keepdims=True)
    return centred * lax.rsqrt(spread + 1e-06) * gain + shift


def exact_gelu(values):
    return jax.nn.gelu(values, approximate=False)


def passage_mask(segment_row, length_row):
    starts = jnp.cumsum(length_row) - length_row
    number = length_row.shape[0]
    onehot = (segment_row[:, None] == jnp.arange(number, dtype=jnp.int32)[None, :]).astype(
        jnp.int32
    )
    opening = jnp.sum(onehot * starts[None, :], axis=1)
    closing = opening + jnp.sum(onehot * length_row[None, :], axis=1)
    places = jnp.arange(segment_row.shape[0], dtype=jnp.int32)
    return (places[None, :] >= opening[:, None]) & (places[None, :] < closing[:, None])


def into_blocks(matrix):
    height, breadth = matrix.shape
    return (
        matrix.reshape(height // BLK, BLK, breadth // BLK, BLK)
        .transpose(0, 2, 1, 3)
        .reshape(-1, BLK, BLK)
    )


def from_blocks(blocks, height, breadth):
    return (
        blocks.reshape(height // BLK, breadth // BLK, BLK, BLK)
        .transpose(0, 2, 1, 3)
        .reshape(height, breadth)
    )


def split_blocks(blocks):
    square = (D // BLK) ** 2
    broad = D * FF // (BLK * BLK)
    w_query = from_blocks(blocks[0:square], D, D)
    w_key = from_blocks(blocks[square : 2 * square], D, D)
    w_value = from_blocks(blocks[2 * square : 3 * square], D, D)
    w_output = from_blocks(blocks[3 * square : 4 * square], D, D)
    w_upward = from_blocks(blocks[4 * square : 4 * square + broad], D, FF)
    w_downward = from_blocks(blocks[4 * square + broad : 4 * square + 2 * broad], FF, D)
    return (w_query, w_key, w_value, w_output, w_upward, w_downward)


def contract_rows(left_mat, right_mat):
    return lax.dot_general(
        left_mat, right_mat, (((0,), (0,)), ((), ())), preferred_element_type=jnp.float32
    )


def contract_cols(left_mat, right_mat):
    return lax.dot_general(
        left_mat, right_mat, (((1,), (1,)), ((), ())), preferred_element_type=jnp.float32
    )


def soap_update(
    gradient, weights, moment_old, second_old, left_old, right_old, left_rot, right_rot
):
    left_next = 0.95 * left_old + 0.05 * jnp.einsum(
        "nij,nkj->nik", gradient, gradient, precision=highest
    )
    right_next = 0.95 * right_old + 0.05 * jnp.einsum(
        "nji,njk->nik", gradient, gradient, precision=highest
    )
    turned = jnp.einsum("nji,njk->nik", left_rot, gradient, precision=highest)
    turned = jnp.einsum("nij,njk->nik", turned, right_rot, precision=highest)
    moment_next = 0.5 * moment_old + 0.5 * turned
    second_next = 0.5 * second_old + 0.5 * turned * turned
    correct = 1.0 - 0.5**STEP
    ratio = moment_next / correct / (jnp.sqrt(second_next / correct) + 1e-08)
    stepped = jnp.einsum("nij,njk->nik", left_rot, ratio, precision=highest)
    stepped = jnp.einsum("nij,nkj->nik", stepped, right_rot, precision=highest)
    return (moment_next, second_next, left_next, right_next, weights - rate_matrix * stepped)


def adam_update(gradient, values, moment_old, second_old):
    moment_next = 0.5 * moment_old + 0.5 * gradient
    second_next = 0.5 * second_old + 0.5 * gradient * gradient
    correct = 1.0 - 0.5**STEP
    ratio = moment_next / correct / (jnp.sqrt(second_next / correct) + 1e-08)
    return (moment_next, second_next, values - rate_vector * ratio)


def masked_scores(joint_row, segment_row, length_row):
    positions = joint_row.shape[0]
    query = joint_row[:, 0].reshape(positions, -1, HD)
    keyed = joint_row[:, 1].reshape(positions, -1, HD)
    valued = joint_row[:, 2].reshape(positions, -1, HD)
    scores = jnp.einsum("qhd,khd->hqk", query, keyed, preferred_element_type=jnp.float32) * 0.125
    visible = passage_mask(segment_row, length_row)
    return (jnp.where(visible[None], scores, -1e30), query, keyed, valued)


def attend_rows(item):
    joint_row, segment_row, length_row = item
    scores, query, keyed, valued = masked_scores(joint_row, segment_row, length_row)
    largest = jnp.max(scores, axis=-1, keepdims=True)
    raised = jnp.exp(scores - largest)
    totals = jnp.sum(raised, axis=-1, keepdims=True)
    probs = raised / totals
    logsum = (largest + jnp.log(totals))[..., 0]
    context = jnp.einsum(
        "hqk,khd->qhd", probs.astype(jnp.bfloat16), valued, preferred_element_type=jnp.float32
    )
    return (context.reshape(joint_row.shape[0], -1).astype(jnp.bfloat16), logsum)


def back_rows(item):
    joint_row, logsum, delta_context, segment_row, length_row = item
    positions = joint_row.shape[0]
    scores, query, keyed, valued = masked_scores(joint_row, segment_row, length_row)
    probs = jnp.exp(scores - logsum[..., None])
    delta_ctx = delta_context.reshape(positions, -1, HD)
    delta_value = jnp.einsum(
        "hqk,qhd->khd", probs.astype(jnp.bfloat16), delta_ctx, preferred_element_type=jnp.float32
    )
    delta_prob = jnp.einsum("qhd,khd->hqk", delta_ctx, valued, preferred_element_type=jnp.float32)
    weighted = jnp.sum(probs * delta_prob, axis=-1, keepdims=True)
    delta_score = (probs * (delta_prob - weighted)).astype(jnp.bfloat16)
    delta_query = (
        jnp.einsum("hqk,khd->qhd", delta_score, keyed, preferred_element_type=jnp.float32) * 0.125
    )
    delta_key = (
        jnp.einsum("hqk,qhd->khd", delta_score, query, preferred_element_type=jnp.float32) * 0.125
    )
    stacked = jnp.stack(
        [
            delta_query.reshape(positions, -1),
            delta_key.reshape(positions, -1),
            delta_value.reshape(positions, -1),
        ],
        axis=1,
    )
    return stacked.astype(jnp.bfloat16)


def pick_blocks(source, slot_index, owner_slot, fanout, part_index):
    matches = owner_slot[None, :] == slot_index[:, None]
    present = jnp.any(matches, axis=1).astype(jnp.float32)
    chosen = jnp.sum(
        matches.astype(jnp.int32) * jnp.arange(owner_slot.shape[0], dtype=jnp.int32)[None, :],
        axis=1,
    )
    picked = jnp.take(source, chosen * fanout + part_index, axis=0)
    return picked * present[:, None, None]


def per_device(
    tokens,
    output_grad,
    segment_ids,
    lengths,
    owner_slot,
    slot_weights,
    first_moment,
    second_moment,
    left_stats,
    right_stats,
    left_basis,
    right_basis,
    vector_values,
    vector_first,
    vector_second,
):
    holding = slot_weights.shape[0]
    row_count = tokens.shape[0]
    token_count = tokens.shape[1]
    gathered, vector_half = (
        lax.all_gather(slot_weights.astype(jnp.bfloat16), "dp", axis=0, tiled=True),
        lax.all_gather(vector_values.astype(jnp.bfloat16), "dp", axis=0, tiled=True),
    )
    blocks = jnp.take(gathered, owner_slot, axis=0)
    w_query, w_key, w_value, w_output, w_upward, w_downward = split_blocks(blocks)
    w_joint = jnp.concatenate([w_query, w_key, w_value], axis=1)
    gains = vector_half.astype(jnp.float32).reshape(4, D)
    flat_tokens = tokens.reshape(-1, D)
    projected = jnp.dot(flat_tokens, w_joint, preferred_element_type=jnp.float32).astype(
        jnp.bfloat16
    )
    projected = projected.reshape(row_count, token_count, 3, D)
    heads = lax.all_to_all(projected, "sp", split_axis=3, concat_axis=1, tiled=True)
    context, logsum = lax.map(attend_rows, (heads, segment_ids, lengths))
    context_tok = lax.all_to_all(context, "sp", split_axis=1, concat_axis=2, tiled=True).reshape(
        -1, D
    )
    attended = jnp.dot(context_tok, w_output, preferred_element_type=jnp.float32)
    summed_one = flat_tokens.astype(jnp.float32) + attended
    hidden, norm_one_pull = jax.vjp(layer_norm, summed_one, gains[0], gains[1])
    hidden_half = hidden.astype(jnp.bfloat16)
    upward = jnp.dot(hidden_half, w_upward, preferred_element_type=jnp.float32)
    activated, gelu_pull = jax.vjp(exact_gelu, upward)
    active_half = activated.astype(jnp.bfloat16)
    downward = jnp.dot(active_half, w_downward, preferred_element_type=jnp.float32)
    result, norm_two_pull = jax.vjp(layer_norm, hidden + downward, gains[2], gains[3])
    block_out = result.astype(jnp.bfloat16).reshape(row_count, token_count, D)
    cotangent = output_grad.reshape(-1, D).astype(jnp.float32)
    delta_two, delta_gain_two, delta_shift_two = norm_two_pull(cotangent)
    delta_down = delta_two.astype(jnp.bfloat16)
    grad_down = contract_rows(active_half, delta_down)
    delta_active = contract_cols(delta_down, w_downward)
    (delta_upward,) = gelu_pull(delta_active)
    delta_up = delta_upward.astype(jnp.bfloat16)
    grad_up = contract_rows(hidden_half, delta_up)
    delta_hidden = delta_two + contract_cols(delta_up, w_upward)
    delta_one, delta_gain_one, delta_shift_one = norm_one_pull(delta_hidden)
    delta_attn = delta_one.astype(jnp.bfloat16)
    grad_output = contract_rows(context_tok, delta_attn)
    delta_context = (
        contract_cols(delta_attn, w_output).astype(jnp.bfloat16).reshape(row_count, token_count, D)
    )
    delta_heads = lax.all_to_all(delta_context, "sp", split_axis=2, concat_axis=1, tiled=True)
    delta_projected = lax.map(back_rows, (heads, logsum, delta_heads, segment_ids, lengths))
    delta_joint = lax.all_to_all(
        delta_projected, "sp", split_axis=1, concat_axis=3, tiled=True
    ).reshape(-1, 3 * D)
    grad_joint = contract_rows(flat_tokens, delta_joint)
    input_grad = (delta_one + contract_cols(delta_joint, w_joint)).reshape(
        row_count, token_count, D
    )
    grad_blocks = jnp.concatenate(
        [
            into_blocks(grad_joint[:, :D]),
            into_blocks(grad_joint[:, D : 2 * D]),
            into_blocks(grad_joint[:, 2 * D :]),
            into_blocks(grad_output),
            into_blocks(grad_up),
            into_blocks(grad_down),
        ],
        axis=0,
    )
    vector_grad = jnp.concatenate(
        [delta_gain_one, delta_shift_one, delta_gain_two, delta_shift_two]
    )
    vector_total = lax.psum(vector_grad, ("dp", "sp"))
    piece_len = vector_values.shape[0]
    vector_piece = lax.dynamic_slice_in_dim(
        vector_total, lax.axis_index("dp") * piece_len, piece_len
    )
    slot_index = jnp.arange(holding * lax.axis_size("dp"), dtype=jnp.int32)
    owned = lax.psum_scatter(
        pick_blocks(grad_blocks, slot_index, owner_slot, 1, 0),
        "dp",
        scatter_dimension=0,
        tiled=True,
    )
    owned = lax.psum(owned.astype(jnp.bfloat16), "sp").astype(jnp.float32)
    moment_one, moment_two, left_new, right_new, weights_new = soap_update(
        owned,
        slot_weights,
        first_moment,
        second_moment,
        left_stats,
        right_stats,
        left_basis,
        right_basis,
    )
    vector_one, vector_two, vector_new = adam_update(
        vector_piece, vector_values, vector_first, vector_second
    )
    return (
        block_out,
        input_grad,
        moment_one,
        moment_two,
        left_new,
        right_new,
        weights_new,
        weights_new.astype(jnp.bfloat16),
        vector_one,
        vector_two,
        vector_new,
    )


def solution(mesh):
    in_specs = (
        P("dp", "sp", None),
        P("dp", "sp", None),
        P("dp", None),
        P("dp", None),
        P(),
        P("dp", None, None),
        P("dp", None, None),
        P("dp", None, None),
        P("dp", None, None),
        P("dp", None, None),
        P("dp", None, None),
        P("dp", None, None),
        P("dp"),
        P("dp"),
        P("dp"),
    )
    out_specs = (
        P("dp", "sp", None),
        P("dp", "sp", None),
        P("dp", None, None),
        P("dp", None, None),
        P("dp", None, None),
        P("dp", None, None),
        P("dp", None, None),
        P("dp", None, None),
        P("dp"),
        P("dp"),
        P("dp"),
    )
    return jax.shard_map(
        per_device, mesh=mesh, in_specs=in_specs, out_specs=out_specs, check_vma=False
    )
```

profile of v0, /device:TPU:1, one launch (start us, length us, event | category | flops | bytes accessed | tf_op | source)
XLA Modules:
  0.0 1260.4 jit_solution(9483962715809352481)
XLA Ops:
  10.9 197.4 %all-gather.3.cloned.1.call-done = bf16[48,384,384]{2,1,0:T(8,128)(2,1)} async-done(((bf16[6,384,384]{2,1,0:T(8,128)(2,1)}), bf16[48,384,384]{2,1,0:T(8,128)(2,1)}) %all-gather.3.cloned.1.call-update) | async-done | bytes 14155792 | tf_op jit(solution)/shard_map/all_gather | solution.py:195
  208.3 12.4 gather_fusion
  220.7 7.8 broadcast_select_fusion
  255.9 21.8 %all-gather = bf16[8,1,384]{2,1,0:T(2,128)(2,1)S(1)} all-gather(bf16[1,1,384]{2,1,0:T(2,128)(2,1)S(1)} %reshape.459), channel_id=1, replica_groups=mesh['dp'=8,'sp'=4] {'dp'}, dimensions={0}, use_global_device_ids=true | all-gather | bytes 6912 | tf_op jit(solution)/shard_map/all_gather | solution.py:196
  293.7 37.0 %while.22 = (s32[]{:T(128)}, bf16[4,512,192]{1,2,0:T(8,128)(2,1)}, f32[4,3,512]{2,1,0:T(4,128)}, bf16[4,512,3,192]{1,3,2,0:T(8,128)(2,1)}, s32[4,512]{1,0:T(4,12...) while((s32[]{:T(128)}, bf16[4,512,192]{1,2,0:T(8,128)(2,1)}, f32[4,3,512]{2,1,0:T(4,128)}, ...), condition=%wide.region_6.7_spmd, body=%wide.region_0.6_spmd.sunk | while | flops 211667008 | bytes 14883321 | solution.py:208
  340.7 7.2 fusion.63
  356.6 7.0 copy.188
  376.2 19.1 %multiply_convert_fusion.1 = (bf16[512,3072]{1,0:T(8,128)(2,1)S(1)}, f32[512,3072]{1,0:T(8,128)S(1)}, f32[512,3072]{1,0:T(8,128)}) fusion(bf16[768,3072]{1,0:T(8,128)(2,1)} %bitcast.311, f32[512,768]{1,0:T(8,128)S(1)} %get-tuple-element.155, f32[768]{0:T(1024)S(1)} %copy-done.45, f32[768]{0:T(1024)S(1)} %reshape.462, f32[512]{0:T(512)S(1)} %fusion.45, ...), kind=kOutput, calls=%fused_computation.51 | convolution fusion | flops 2520121344 | bytes 22030336 | tf_op jit(solution)/shard_map/dot_general | solution.py:216
  401.3 7.4 add_convert_fusion
  426.3 6.9 all-to-all-done.2
  435.4 79.8 %while.23 = (s32[]{:T(128)}, bf16[4,512,3,192]{1,3,2,0:T(8,128)(2,1)}, bf16[4,512,3,192]{1,3,2,0:T(8,128)(2,1)}, s32[4,512]{1,0:T(4,128)}, s32[4,8]{1,0:T(4,128)...) while((s32[]{:T(128)}, bf16[4,512,3,192]{1,3,2,0:T(8,128)(2,1)}, ...), condition=%wide.region_20.21_spmd, body=%wide.region_15.20_spmd.sunk | while | flops 513460288 | bytes 45795956 | solution.py:238
  531.7 8.9 fusion.53
  557.3 12.5 reshape.439
  569.8 8.6 copy.199
  580.6 7.1 copy.193
  633.0 8.7 constant_dynamic-update-slice_fusion.5
  646.0 21.1 %gather_fusion.1 = f32[48,384,384]{2,1,0:T(8,128)} fusion(f32[48,384,384]{2,1,0:T(8,128)} %constant_dynamic-update-slice_fusion.4, s32[1024]{0:T(1024)} %pad_clamp_fusion), kind=kCustom, calls=%fused_computation.1 | custom fusion | bytes 56623296 | tf_op jit(solution)/shard_map/jit(_take)/gather | solution.py:170
  667.1 27.7 %copy.200 = f32[48,384,384]{1,2,0:T(8,128)} copy(f32[48,384,384]{2,1,0:T(8,128)} %gather_fusion.1) | data formatting | bytes 56623104 | tf_op jit(solution)/shard_map/jit(_take)/gather | solution.py:170
  694.8 20.7 %select_multiply_fusion = f32[48,384,384]{1,2,0:T(8,128)} fusion(f32[48,384,384]{1,2,0:T(8,128)} %copy.200, f32[48]{0:T(128)S(1)} %copy-done.48, pred[48]{0:T(512)(128)(4,1)S(1)} %copy-done.49), kind=kLoop, calls=%fused_computation.46 | loop fusion | flops 14155776 | bytes 56623344 | tf_op jit(solution)/shard_map/mul | solution.py:171
  717.7 445.0 %reduce-scatter.2.cloned.1.call-done = f32[6,384,384]{1,2,0:T(8,128)} async-done(((f32[48,384,384]{1,2,0:T(8,128)}), f32[6,384,384]{1,2,0:T(8,128)}) %reduce-scatter.2.cloned.1.call-update) | async-done | bytes 3538960 | tf_op jit(solution)/shard_map/reduce_scatter | solution.py:266
  1166.1 40.6 %psum.15 = f32[3072]{0:T(1024)} all-reduce(f32[3072]{0:T(1024)S(1)} %pad_maximum_fusion), channel_id=1, replica_groups=mesh['dp'=8,'sp'=4] {'dp','sp'}, use_global_device_ids=true, to_apply=%region_29.30 | all-reduce | flops 3072 | bytes 24576 | tf_op jit(solution)/shard_map/psum | solution.py:260
  1221.0 8.3 fusion.22
  1229.3 8.7 fusion.23
  1238.1 9.1 fusion.68
  (409 shorter events, 331.5 us)
Async XLA Ops:
  7.2 1213.8 %copy-start = (f32[6,384,384]{2,1,0:T(8,128)S(1)}, f32[6,384,384]{2,1,0:T(8,128)}, u32[]{:S(2)}) copy-start(f32[6,384,384]{2,1,0:T(8,128)} %param.30) | copy-start | bytes 10616836
  7.2 201.1 %all-gather.3.cloned.1.call-start = ((), (), s32[]{:S(2)}) async-start(), calls=%async_computation.5 | async-start | bytes 15925248 | tf_op jit(solution)/shard_map/all_gather | solution.py:195
  250.2 33.4 %all-to-all-start = ((bf16[4,128,3,768]{1,0,2,3:T(4,128)(2,1)}), bf16[4,128,3,768]{1,0,2,3:T(4,128)(2,1)}, u32[]{:S(2)}, u32[]{:S(2)}) async-start(bf16[4,128,3,768]{1,0,2,3:T(4,128)(2,1)} %copy.182), calls=%async_computation | async-start | bytes 4718592 | tf_op jit(solution)/shard_map/all_to_all | solution.py:207
  330.7 9.3 copy-start.37
  330.7 9.3 copy-start.36
  330.7 9.4 copy-start.35
  333.1 36.2 %all-to-all-start.1 = ((bf16[4,512,192]{2,0,1:T(4,128)(2,1)}), bf16[4,512,192]{2,0,1:T(4,128)(2,1)}, u32[]{:S(2)}, u32[]{:S(2)}) async-start(bf16[4,512,192]{2,0,1:T(4,128)(2,1)} %copy.184), calls=%async_computation.1 | async-start | bytes 2097152 | tf_op jit(solution)/shard_map/all_to_all | solution.py:209
  340.1 55.2 %copy-start.31 = (f32[768]{0:T(1024)}, f32[768]{0:T(1024)S(1)}, u32[]{:S(2)}) copy-start(f32[768]{0:T(1024)S(1)} %reshape.462) | copy-start | bytes 9220
  373.0 22.2 %slice-start.5 = ((s8[4718592]{0:T(1024)(128)(4,1)}), s8[4194304]{0:T(1024)(128)(4,1)S(1)}, s32[]{:S(2)}) async-start(s8[4718592]{0:T(1024)(128)(4,1)} %bitcast.315), calls=%async_computation.13 | async-start | bytes 8388608
  375.8 36.6 %copy-start.12 = (f32[512,768]{1,0:T(8,128)}, f32[512,768]{1,0:T(8,128)S(1)}, u32[]{:S(2)}) copy-start(f32[512,768]{1,0:T(8,128)S(1)} %get-tuple-element.155) | copy-start | bytes 4718596
  376.1 36.2 %copy-start.39 = (f32[512]{0:T(512)}, f32[512]{0:T(512)S(1)}, u32[]{:S(2)}) copy-start(f32[512]{0:T(512)S(1)} %fusion.45) | copy-start | bytes 6148
  376.1 19.1 %slice-start.6 = ((s8[4718592]{0:T(1024)(128)(4,1)}), s8[524288]{0:T(1024)(128)(4,1)S(1)}, s32[]{:S(2)}) async-start(s8[4718592]{0:T(1024)(128)(4,1)} %bitcast.315), calls=%async_computation.14 | async-start | bytes 1048576
  399.6 9.1 slice-start.3
  418.0 15.1 %all-to-all-start.2 = ((bf16[4,128,768]{1,0,2:T(4,128)(2,1)}), bf16[4,128,768]{1,0,2:T(4,128)(2,1)}, u32[]{:S(2)}, u32[]{:S(2)}) async-start(bf16[4,128,768]{1,0,2:T(4,128)(2,1)} %copy.189), calls=%async_computation.2 | async-start | bytes 1572864 | tf_op jit(solution)/shard_map/all_to_all | solution.py:237
  520.9 59.7 %all-to-all-start.3 = ((bf16[4,512,3,192]{3,0,2,1:T(4,128)(2,1)}), bf16[4,512,3,192]{3,0,2,1:T(4,128)(2,1)}, u32[]{:S(2)}, u32[]{:S(2)}) async-start(bf16[4,512,3,192]{3,0,2,1:T(4,128)(2,1)} %copy.192), calls=%async_computation.3 | async-start | bytes 6291456 | tf_op jit(solution)/shard_map/all_to_all | solution.py:239
  526.5 636.1 %reduce-scatter.2.cloned.1.call-start = ((), (), s32[]{:S(2)}) async-start(), calls=%async_computation.6 | async-start | bytes 31850496 | tf_op jit(solution)/shard_map/reduce_scatter | solution.py:266
  631.4 10.3 slice-start
  667.1 27.7 %copy-start.48 = (f32[48]{0:T(128)S(1)}, f32[48]{0:T(128)}, u32[]{:S(2)}) copy-start(f32[48]{0:T(128)} %convert_element_type.113) | copy-start | bytes 580
  667.1 27.7 %copy-start.49 = (pred[48]{0:T(512)(128)(4,1)S(1)}, pred[48]{0:T(512)(128)(4,1)}, u32[]{:S(2)}) copy-start(pred[48]{0:T(512)(128)(4,1)} %compare_and_fusion) | copy-start | bytes 148
  715.6 498.8 %all-reduce.2.cloned.1.call-start = ((), (), s32[]{:S(2)}) async-start(), calls=%async_computation.7 | async-start | bytes 3538944 | tf_op jit(solution)/shard_map/psum | solution.py:272
  717.7 489.0 %copy-start.42 = (f32[384]{0:T(512)S(1)}, f32[384]{0:T(512)}, u32[]{:S(2)}) copy-start(f32[384]{0:T(512)} %param.31) | copy-start | bytes 4612
  1229.3 8.8 copy-start.21
  1238.1 9.1 copy-start.5
  1238.1 9.1 copy-start.17
  (65 other events, 268.4 us)
Sparse Core Ops, SparseCore 0:
  11.0 197.2 all-gather.2
  715.7 446.8 reduce-scatter.1
  1166.2 45.9 all-reduce.1
where the time goes:
time: 1270 us; the launch traced here: 1260 us
  waiting for transfers between devices  655 us (52%)
  local copies, waits for them, and re-layouts  283 us (22%)
  matrix products  147 us (12%)
  other arithmetic  77.1 us (6%)
  blocking collectives  62.4 us (5%)
  starting transfers between devices  21.1 us (2%)
  between operations  14.6 us (1%)
    reduce_scatter x1, waiting for transfers between devices, per_device(): lax.psum_scatter(pick_blocks(grad_blocks, slot_index, owner_slot, 1, 0),...  445 us
    all_gather x1, waiting for transfers between devices, per_device(): lax.all_gather(slot_weights.astype(jnp.bfloat16), 'dp', axis=0, tiled=True)  197 us
    reshape x9, local copies, waits for them, and re-layouts, into_blocks(): matrix.reshape(height // BLK, BLK, breadth // BLK, BLK)  54 us
    gather x2, local copies, waits for them, and re-layouts, pick_blocks(): picked = jnp.take(source, chosen * fanout + part_index, axis=0)  48.8 us
    unnamed x132, local copies, waits for them, and re-layouts  42.7 us
    psum x1, blocking collectives, per_device(): vector_total = lax.psum(vector_grad, ('dp', 'sp'))  40.6 us
  transfers between devices with their start and end apart: 7, of which 4 were waited for; matrix products, arithmetic and copies ran while one was open for 8% of the time, Pallas kernels for 0%

commit v1 on v0

--- a/solution.py
+++ b/solution.py
@@ -1,6 +1,9 @@
+import functools
 import jax
 import jax.numpy as jnp
 from jax import lax
+from jax.experimental import pallas as pl
+from jax.experimental.pallas import tpu as pltpu
 from jax.sharding import PartitionSpec as P
 
 D = 768
@@ -298,6 +301,590 @@
     )
 
 
+PITCH = BLK + 16
+MESH = pl.DeviceIdType.MESH
+NZ = 4
+
+
+def place():
+    dp = lax.axis_index("dp")
+    sp = lax.axis_index("sp")
+    return dp // 2, dp % 2, sp // 2, sp % 2
+
+
+def greet(z, y, x, c):
+    barrier = pltpu.get_barrier_semaphore()
+    dp = z * 2 + y
+    sp = x * 2 + c
+
+    def signal(target):
+        pl.semaphore_signal(barrier, 1, device_id=target, device_id_type=MESH)
+
+    for step in range(1, 4):
+        signal((dp, (sp + step) % 4))
+    signal((z * 2 + 1 - y, sp))
+
+    @pl.when(z < NZ - 1)
+    def _():
+        signal((dp + 2, sp))
+
+    @pl.when(z > 0)
+    def _():
+        signal((dp - 2, sp))
+
+    pl.semaphore_wait(barrier, 4 + (z < NZ - 1).astype(jnp.int32) + (z > 0).astype(jnp.int32))
+
+
+def gather_kernel(
+    weights, vector, tokens, grads, out, token_row, grad_row,
+    wide, narrow, load_sem, keep_sem, send_sem, recv_sem, row_send, row_recv, row_keep,
+):
+    z, y, x, c = place()
+    dp = z * 2 + y
+    sp = x * 2 + c
+    loads = [pltpu.make_async_copy(weights.at[i], wide.at[i], load_sem.at[i]) for i in range(6)]
+    for load in loads:
+        load.start()
+    keeps = [
+        pltpu.make_async_copy(tokens.at[sp], token_row.at[sp], row_keep.at[0]),
+        pltpu.make_async_copy(grads.at[sp], grad_row.at[sp], row_keep.at[1]),
+    ]
+    for keep in keeps:
+        keep.start()
+    gains = jnp.broadcast_to(vector[...], (16, BLK)).astype(jnp.bfloat16)
+    greet(z, y, x, c)
+
+    def rows_copy(which, source, landing, step):
+        peer = (sp + step) % 4
+        return pltpu.make_async_remote_copy(
+            src_ref=source.at[peer], dst_ref=landing.at[sp],
+            send_sem=row_send.at[which, step - 1], recv_sem=row_recv.at[which, sp],
+            device_id=(dp, peer), device_id_type=MESH,
+        )
+
+    def rows_arrival(which, source, landing, step):
+        peer = (sp + step) % 4
+        return pltpu.make_async_remote_copy(
+            src_ref=source.at[peer], dst_ref=landing.at[peer],
+            send_sem=row_send.at[which, step - 1], recv_sem=row_recv.at[which, peer],
+            device_id=(dp, peer), device_id_type=MESH,
+        )
+
+    for step in (2, 3, 1):
+        rows_copy(0, tokens, token_row, step).start()
+
+    for i in range(6):
+        loads[i].wait()
+        narrow[i, :BLK, :] = wide[i].astype(jnp.bfloat16)
+        narrow[i, BLK:, :] = gains
+    own = [pltpu.make_async_copy(narrow.at[i], out.at[dp * 6 + i], keep_sem.at[i]) for i in range(6)]
+
+    def piece(part):
+        return (c, BLK + 16) if part == 0 else (2 + 2 * x + c, BLK)
+
+    targets = {
+        "up": (dp + 2, sp), "down": (dp - 2, sp), "y": (z * 2 + 1 - y, sp),
+        "x": (dp, (1 - x) * 2 + c), "core": (dp, x * 2 + 1 - c),
+    }
+    number = {"up": 0, "down": 1, "y": 2, "x": 3, "core": 4}
+
+    def copy(way, holder, slot, height, index, source=None):
+        at = holder * 6 + slot
+        src = out.at[at, pl.ds(0, height)] if source is None else source
+        return pltpu.make_async_remote_copy(
+            src_ref=src, dst_ref=out.at[at, pl.ds(0, height)],
+            send_sem=send_sem.at[number[way], index], recv_sem=recv_sem.at[at],
+            device_id=targets[way], device_id_type=MESH,
+        )
+
+    started = []
+
+    def start(way, holder, slot, height, index, valid=None, source=None):
+        item = copy(way, holder, slot, height, index, source)
+        if valid is None:
+            item.start()
+        else:
+            pl.when(valid)(item.start)
+        started.append((item, valid))
+
+    def arrive(holder, slot, height, valid=None):
+        item = copy("core", holder, slot, height, 0)
+        if valid is None:
+            item.wait_recv()
+        else:
+            pl.when(valid)(item.wait_recv)
+
+    counts = {}
+
+    def fresh(way):
+        counts[way] = counts.get(way, -1) + 1
+        return counts[way]
+
+    for part in (1, 0):
+        slot, height = piece(part)
+        src = narrow.at[slot, pl.ds(0, height)]
+        start("up", dp, slot, height, fresh("up"), z < NZ - 1, src)
+        start("down", dp, slot, height, fresh("down"), z > 0, src)
+        start("y", dp, slot, height, fresh("y"), None, src)
+    for item in own:
+        item.start()
+
+    def from_z(sign, far, part):
+        origin = z + sign * far
+        inside = (origin >= 0) if sign < 0 else (origin <= NZ - 1)
+        holder = origin * 2 + y
+        slot, height = piece(part)
+        arrive(holder, slot, height, inside)
+        if far < NZ - 1:
+            if sign < 0:
+                start("up", holder, slot, height, fresh("up"), inside & (z < NZ - 1))
+            else:
+                start("down", holder, slot, height, fresh("down"), inside & (z > 0))
+        start("y", holder, slot, height, fresh("y"), inside)
+        if part == 1:
+            start("x", holder, slot, height, fresh("x"), inside)
+        start("core", holder, slot, height, fresh("core"), inside)
+
+    def signs(far):
+        return (0,) if far == 0 else (-1, 1)
+
+    def valid_of(sign, far):
+        origin = z + sign * far
+        if far == 0:
+            return origin, None
+        return origin, ((origin >= 0) if sign < 0 else (origin <= NZ - 1))
+
+    def from_y(sign, far, part):
+        origin, inside = valid_of(sign, far)
+        holder = origin * 2 + 1 - y
+        slot, height = piece(part)
+        arrive(holder, slot, height, inside)
+        if part == 1:
+            start("x", holder, slot, height, fresh("x"), inside)
+        start("core", holder, slot, height, fresh("core"), inside)
+
+    def from_x(sign, far, side):
+        origin, inside = valid_of(sign, far)
+        holder = origin * 2 + (y if side == 0 else 1 - y)
+        slot = 2 + 2 * (1 - x) + c
+        arrive(holder, slot, BLK, inside)
+        start("core", holder, slot, BLK, fresh("core"), inside)
+
+    for far in range(1, NZ):
+        for part in (1, 0):
+            for sign in (-1, 1):
+                from_z(sign, far, part)
+            for sign in signs(far - 1):
+                from_y(sign, far - 1, part)
+        if far == 1:
+            for step in (2, 3, 1):
+                rows_copy(1, grads, grad_row, step).start()
+        if far >= 2:
+            for sign in signs(far - 1):
+                from_x(sign, far - 1, 0)
+            for sign in signs(far - 2):
+                from_x(sign, far - 2, 1)
+    for part in (1, 0):
+        for sign in (-1, 1):
+            from_y(sign, NZ - 1, part)
+    for sign in (-1, 1):
+        from_x(sign, NZ - 1, 0)
+    for far in (NZ - 2, NZ - 1):
+        for sign in signs(far):
+            from_x(sign, far, 1)
+
+    for far in range(NZ):
+        for sign in signs(far):
+            origin, inside = valid_of(sign, far)
+            for side in (0, 1):
+                if far == 0 and side == 0:
+                    continue
+                holder = origin * 2 + (y if side == 0 else 1 - y)
+                for slot, height in ((1 - c, BLK + 16), (3 - c, BLK), (5 - c, BLK)):
+                    arrive(holder, slot, height, inside)
+    for step in (2, 3, 1):
+        rows_arrival(0, tokens, token_row, step).wait_recv()
+        rows_arrival(1, grads, grad_row, step).wait_recv()
+        rows_copy(0, tokens, token_row, step).wait_send()
+        rows_copy(1, grads, grad_row, step).wait_send()
+    for item, valid in started:
+        if valid is None:
+            item.wait_send()
+        else:
+            pl.when(valid)(item.wait_send)
+    for item in own + keeps:
+        item.wait()
+
+
+def gather_all(weights, vector, tokens, grads):
+    anywhere = pl.BlockSpec(memory_space=pl.ANY)
+    return pl.pallas_call(
+        gather_kernel,
+        name="gather_all",
+        out_shape=[
+            jax.ShapeDtypeStruct((48, PITCH, BLK), jnp.bfloat16),
+            jax.ShapeDtypeStruct(tokens.shape, jnp.bfloat16),
+            jax.ShapeDtypeStruct(grads.shape, jnp.bfloat16),
+        ],
+        in_specs=[anywhere, pl.BlockSpec(memory_space=pltpu.VMEM), anywhere, anywhere],
+        out_specs=[anywhere, anywhere, anywhere],
+        scratch_shapes=[
+            pltpu.VMEM((6, BLK, BLK), jnp.float32),
+            pltpu.VMEM((6, PITCH, BLK), jnp.bfloat16),
+            pltpu.SemaphoreType.DMA((6,)),
+            pltpu.SemaphoreType.DMA((6,)),
+            pltpu.SemaphoreType.DMA((5, 40)),
+            pltpu.SemaphoreType.DMA((48,)),
+            pltpu.SemaphoreType.DMA((2, 3)),
+            pltpu.SemaphoreType.DMA((2, 4)),
+            pltpu.SemaphoreType.DMA((2,)),
+        ],
+        compiler_params=pltpu.CompilerParams(
+            collective_id=0, has_side_effects=True, vmem_limit_bytes=24 << 20
+        ),
+    )(weights, vector.reshape(1, BLK), tokens, grads)
+
+
+BLANK = BLK + 16
+HALF = BLK // 2
+
+
+def reduce_kernel(
+    grads, rows_a, rows_b, total, land_a, land_b,
+    mine0, mine1, mine2, mine3, core0, core1, core2, core3, cross, side0, side1, side2,
+    line0, line1, line2, last0, last1,
+    load_sem, core_send, core_recv, x_send, x_recv, y_send, y_recv, z_send, z_recv,
+    last_send, last_recv, give_send, give_recv, keep_sem, row_send, row_recv, row_keep,
+):
+    z, y, x, c = place()
+    dp = z * 2 + y
+    sp = x * 2 + c
+    mine = (mine0, mine1, mine2, mine3)
+    core = (core0, core1, core2, core3)
+    side = (side0, side1, side2)
+    line = (line0, line1, line2)
+    last = (last0, last1)
+    high = z // 2
+    order = (3 - 3 * high, 2 - high, 1 - z + 4 * high, z)
+    twin = (dp, (1 - x) * 2 + c)
+    mate = (dp, x * 2 + 1 - c)
+    beside = (z * 2 + 1 - y, sp)
+    inner = (z > 0) & (z < NZ - 1)
+
+    def view(ref, stream, dest, core_of):
+        base = dest * 6
+        if stream == 0:
+            return ref.at[base + core_of, pl.ds(0, BLANK)]
+        if stream == 1:
+            return ref.at[base + 2 + core_of, pl.ds(0, BLK)]
+        slot = base + (4 + x if stream == 2 else 5 - x)
+        return ref.at[slot, pl.ds(pl.multiple_of(core_of * HALF, HALF), HALF)]
+
+    def remote(src, dst, send, recv, target):
+        return pltpu.make_async_remote_copy(
+            src_ref=src, dst_ref=dst, send_sem=send, recv_sem=recv,
+            device_id=target, device_id_type=MESH,
+        )
+
+    def load(stream, dest):
+        return pltpu.make_async_copy(
+            view(grads, stream, dest, c), mine[stream].at[dest], load_sem.at[stream, dest]
+        )
+
+    def to_mate(stream, dest):
+        return remote(
+            view(grads, stream, dest, 1 - c), core[stream].at[dest],
+            core_send.at[stream, dest], core_recv.at[stream, dest], mate,
+        )
+
+    def to_twin(dest):
+        return remote(mine3.at[dest], cross.at[dest], x_send.at[dest], x_recv.at[dest], twin)
+
+    def to_side(stream, goal):
+        dest = goal * 2 + 1 - y
+        return remote(
+            mine[stream].at[dest], side[stream].at[goal],
+            y_send.at[stream, goal], y_recv.at[stream, goal], beside,
+        )
+
+    def row_copy(which, source, landing, step, arrival):
+        peer = (sp + step) % 4
+        at = peer if arrival else sp
+        return remote(
+            source.at[peer], landing.at[at],
+            row_send.at[which, step - 1], row_recv.at[which, at], (dp, peer),
+        )
+
+    sequence = []
+    for i in range(4):
+        away = order[i] * 2 + 1 - y
+        sequence += [(3, away), (0, away), (1, away)]
+    for i in range(4):
+        sequence += [(3, order[i] * 2 + y)]
+    for i in range(4):
+        sequence += [(2, order[i] * 2 + 1 - y)]
+    for i in range(4):
+        home = order[i] * 2 + y
+        sequence += [(0, home), (1, home)]
+    for i in range(4):
+        sequence += [(2, order[i] * 2 + y)]
+    for stream, dest in sequence:
+        load(stream, dest).start()
+    keeps = [
+        pltpu.make_async_copy(rows_a.at[sp], land_a.at[sp], row_keep.at[0]),
+        pltpu.make_async_copy(rows_b.at[sp], land_b.at[sp], row_keep.at[1]),
+    ]
+    for keep in keeps:
+        keep.start()
+    greet(z, y, x, c)
+    for stream, dest in sequence:
+        to_mate(stream, dest).start()
+
+    def merge(stream, dest):
+        load(stream, dest).wait()
+        to_mate(stream, dest).wait_recv()
+        mine[stream][dest] = mine[stream][dest] + core[stream][dest]
+
+    def along(stream, goal):
+        dest = goal * 2 + y
+        upward = (goal > z).astype(jnp.int32)
+        step = 2 * upward - 1
+        way = 1 - upward
+        item = remote(
+            mine[stream].at[dest], line[stream].at[way, goal],
+            z_send.at[stream, goal], z_recv.at[stream, way, goal], (dp + 2 * step, sp),
+        )
+
+        @pl.when(inner)
+        def _():
+            item.wait_recv()
+            mine[stream][dest] = mine[stream][dest] + line[stream][way, goal]
+
+        item.start()
+
+    def settle(stream):
+        for way, valid, step in ((0, z > 0, 1), (1, z < NZ - 1, -1)):
+            @pl.when(valid)
+            def _():
+                remote(
+                    mine[stream].at[dp], line[stream].at[way, z],
+                    z_send.at[stream, z], z_recv.at[stream, way, z], (dp - 2 * step, sp),
+                ).wait_recv()
+                mine[stream][dp] = mine[stream][dp] + line[stream][way, z]
+
+    for i in range(4):
+        away = order[i] * 2 + 1 - y
+        merge(3, away)
+        to_twin(away).start()
+        for stream in (0, 1):
+            merge(stream, away)
+            to_side(stream, order[i]).start()
+    for i in range(4):
+        home = order[i] * 2 + y
+        merge(3, home)
+        to_twin(home).start()
+    for step in (2, 3, 1):
+        row_copy(0, rows_a, land_a, step, False).start()
+    for i in range(4):
+        away = order[i] * 2 + 1 - y
+        merge(2, away)
+        to_twin(away).wait_recv()
+        mine2[away] = mine2[away] + cross[away]
+        to_side(2, order[i]).start()
+        home = order[i] * 2 + y
+        for stream in (0, 1):
+            merge(stream, home)
+            to_side(stream, order[i]).wait_recv()
+            mine[stream][home] = mine[stream][home] + side[stream][order[i]]
+            if i < 3:
+                along(stream, order[i])
+    for step in (2, 3, 1):
+        row_copy(1, rows_b, land_b, step, False).start()
+    for i in range(4):
+        home = order[i] * 2 + y
+        merge(2, home)
+        to_twin(home).wait_recv()
+        mine2[home] = mine2[home] + cross[home]
+        to_side(2, order[i]).wait_recv()
+        mine2[home] = mine2[home] + side2[order[i]]
+        if i < 3:
+            along(2, order[i])
+
+    def swap_last(stream):
+        return remote(
+            mine[stream].at[dp], last[stream], last_send.at[stream], last_recv.at[stream], twin
+        )
+
+    for stream in (0, 1):
+        settle(stream)
+        swap_last(stream).start()
+    settle(2)
+
+    def place_of(stream, core_of):
+        return view(total, stream, 0, core_of)
+
+    def give(stream, index, target, source, core_of):
+        return remote(
+            source, place_of(stream, core_of), give_send.at[index], give_recv.at[index], target
+        )
+
+    own_twin = give(2, 0, twin, mine2.at[dp], c)
+    own_twin.start()
+    own_mate = give(2, 1, mate, mine2.at[dp], c)
+    own_mate.start()
+    kept = [pltpu.make_async_copy(mine2.at[dp], place_of(2, c), keep_sem.at[2])]
+    kept[0].start()
+    gifts = [own_twin, own_mate]
+    for stream in (0, 1):
+        swap_last(stream).wait_recv()
+        core[stream][dp] = mine[stream][dp] + last[stream][...]
+        gift = give(stream, 2 + stream, mate, core[stream].at[dp], c)
+        gift.start()
+        gifts.append(gift)
+        keep = pltpu.make_async_copy(core[stream].at[dp], place_of(stream, c), keep_sem.at[stream])
+        keep.start()
+        kept.append(keep)
+    give(3, 0, twin, place_of(3, c), c).wait_recv()
+    passed = give(3, 4, mate, place_of(3, c), c)
+    passed.start()
+    gifts.append(passed)
+    for stream, index in ((2, 1), (0, 2), (1, 3), (3, 4)):
+        give(stream, index, mate, place_of(stream, 1 - c), 1 - c).wait_recv()
+    for step in (2, 3, 1):
+        for which, source, landing in ((0, rows_a, land_a), (1, rows_b, land_b)):
+            row_copy(which, source, landing, step, True).wait_recv()
+            row_copy(which, source, landing, step, False).wait_send()
+    for stream, dest in sequence:
+        to_mate(stream, dest).wait_send()
+    for i in range(4):
+        for side_of in (0, 1):
+            to_twin(order[i] * 2 + side_of).wait_send()
+        for stream in range(3):
+            to_side(stream, order[i]).wait_send()
+            if i < 3:
+                remote(
+                    mine[stream].at[order[i] * 2 + y], line[stream].at[0, order[i]],
+                    z_send.at[stream, order[i]], z_recv.at[stream, 0, order[i]], twin,
+                ).wait_send()
+    for stream in (0, 1):
+        swap_last(stream).wait_send()
+    for item in gifts:
+        item.wait_send()
+    for item in kept + keeps:
+        item.wait()
+
+
+def reduce_all(grads, rows_a, rows_b):
+    anywhere = pl.BlockSpec(memory_space=pl.ANY)
+    half = jnp.bfloat16
+    heights = (BLANK, BLK, HALF, HALF)
+    dma = pltpu.SemaphoreType.DMA
+    return pl.pallas_call(
+        reduce_kernel,
+        name="reduce_all",
+        out_shape=[
+            jax.ShapeDtypeStruct((6, PITCH, BLK), half),
+            jax.ShapeDtypeStruct(rows_a.shape, half),
+            jax.ShapeDtypeStruct(rows_b.shape, half),
+        ],
+        in_specs=[anywhere] * 3,
+        out_specs=[anywhere] * 3,
+        scratch_shapes=[pltpu.VMEM((8, h, BLK), half) for h in heights]
+        + [pltpu.VMEM((8, h, BLK), half) for h in heights]
+        + [pltpu.VMEM((8, HALF, BLK), half)]
+        + [pltpu.VMEM((4, h, BLK), half) for h in heights[:3]]
+        + [pltpu.VMEM((2, 4, h, BLK), half) for h in heights[:3]]
+        + [pltpu.VMEM((h, BLK), half) for h in heights[:2]]
+        + [
+            dma((4, 8)), dma((4, 8)), dma((4, 8)), dma((8,)), dma((8,)), dma((3, 4)), dma((3, 4)),
+            dma((3, 4)), dma((3, 2, 4)), dma((2,)), dma((2,)), dma((5,)), dma((5,)), dma((3,)),
+            dma((2, 3)), dma((2, 4)), dma((2,)),
+        ],
+        compiler_params=pltpu.CompilerParams(
+            collective_id=1, has_side_effects=True, vmem_limit_bytes=30 << 20
+        ),
+    )(grads, rows_a, rows_b)
+
+
+def attend_dense(joint, segment_row, length_row):
+    return attend_rows((joint, segment_row, length_row))
+
+
+def fast_device(
+    tokens, output_grad, segment_ids, lengths, owner_slot, slot_weights, first_moment, second_moment,
+    left_stats, right_stats, left_basis, right_basis, vector_values, vector_first, vector_second,
+):
+    row_count, token_count = tokens.shape[0], tokens.shape[1]
+    place_sp = lax.axis_index("sp")
+    gathered, token_row, grad_row = gather_all(slot_weights, vector_values, tokens, output_grad)
+    gains = gathered[::6, BLK].reshape(4, D).astype(jnp.float32)
+    segment_row = lax.dynamic_index_in_dim(segment_ids, place_sp, 0, False)
+    length_row = lax.dynamic_index_in_dim(lengths, place_sp, 0, False)
+    blocks = jnp.take(gathered, owner_slot, axis=0)[:, :BLK]
+    w_query, w_key, w_value, w_output, w_upward, w_downward = split_blocks(blocks)
+    w_joint = jnp.concatenate([w_query, w_key, w_value], axis=1)
+    flat_tokens = token_row.reshape(-1, D)
+    count = flat_tokens.shape[0]
+    projected = jnp.dot(flat_tokens, w_joint, preferred_element_type=jnp.float32).astype(jnp.bfloat16)
+    joint = projected.reshape(count, 3, D)
+    context_tok, logsum = attend_rows((joint, segment_row, length_row))
+    attended = jnp.dot(context_tok, w_output, preferred_element_type=jnp.float32)
+    summed_one = flat_tokens.astype(jnp.float32) + attended
+    hidden, norm_one_pull = jax.vjp(layer_norm, summed_one, gains[0], gains[1])
+    hidden_half = hidden.astype(jnp.bfloat16)
+    upward = jnp.dot(hidden_half, w_upward, preferred_element_type=jnp.float32)
+    activated, gelu_pull = jax.vjp(exact_gelu, upward)
+    active_half = activated.astype(jnp.bfloat16)
+    downward = jnp.dot(active_half, w_downward, preferred_element_type=jnp.float32)
+    result, norm_two_pull = jax.vjp(layer_norm, hidden + downward, gains[2], gains[3])
+    block_row = result.astype(jnp.bfloat16)
+    cotangent = grad_row.reshape(-1, D).astype(jnp.float32)
+    delta_two, delta_gain_two, delta_shift_two = norm_two_pull(cotangent)
+    delta_down = delta_two.astype(jnp.bfloat16)
+    grad_down = contract_rows(active_half, delta_down)
+    (delta_upward,) = gelu_pull(contract_cols(delta_down, w_downward))
+    delta_up = delta_upward.astype(jnp.bfloat16)
+    grad_up = contract_rows(hidden_half, delta_up)
+    delta_hidden = delta_two + contract_cols(delta_up, w_upward)
+    delta_one, delta_gain_one, delta_shift_one = norm_one_pull(delta_hidden)
+    delta_attn = delta_one.astype(jnp.bfloat16)
+    grad_output = contract_rows(context_tok, delta_attn)
+    delta_context = contract_cols(delta_attn, w_output).astype(jnp.bfloat16)
+    delta_joint = back_rows((joint, logsum, delta_context, segment_row, length_row)).reshape(-1, 3 * D)
+    grad_joint = contract_rows(flat_tokens, delta_joint)
+    input_row = (delta_one + contract_cols(delta_joint, w_joint)).astype(jnp.bfloat16)
+    grad_blocks = jnp.concatenate(
+        [
+            into_blocks(grad_joint[:, :D]),
+            into_blocks(grad_joint[:, D : 2 * D]),
+            into_blocks(grad_joint[:, 2 * D :]),
+            into_blocks(grad_output),
+            into_blocks(grad_up),
+            into_blocks(grad_down),
+        ],
+        axis=0,
+    ).astype(jnp.bfloat16)
+    vector_grad = jnp.concatenate([delta_gain_one, delta_shift_one, delta_gain_two, delta_shift_two])
+    slot_index = jnp.arange(48, dtype=jnp.int32)
+    placed = pick_blocks(grad_blocks, slot_index, owner_slot, 1, 0).astype(jnp.bfloat16)
+    extra = jnp.broadcast_to(
+        vector_grad.astype(jnp.bfloat16).reshape(8, 1, 1, BLK), (8, 6, 16, BLK)
+    ).reshape(48, 16, BLK)
+    placed = jnp.concatenate([placed, extra], axis=1)
+    rows_of = lambda row: row.reshape(row_count, token_count, D)
+    total, block_out, input_half = reduce_all(placed, rows_of(block_row), rows_of(input_row))
+    owned = total[:, :BLK].astype(jnp.float32)
+    vector_piece = total[0, BLK].astype(jnp.float32)
+    moment_one, moment_two, left_new, right_new, weights_new = soap_update(
+        owned, slot_weights, first_moment, second_moment, left_stats, right_stats, left_basis, right_basis
+    )
+    vector_one, vector_two, vector_new = adam_update(vector_piece, vector_values, vector_first, vector_second)
+    return (
+        block_out, input_half.astype(jnp.float32), moment_one, moment_two, left_new, right_new, weights_new,
+        weights_new.astype(jnp.bfloat16), vector_one, vector_two, vector_new,
+    )
+
+
 def solution(mesh):
     in_specs = (
         P("dp", "sp", None),
@@ -329,6 +916,7 @@
         P("dp"),
         P("dp"),
     )
+    chosen = fast_device if dict(mesh.shape) == {"dp": 8, "sp": 4} else per_device
     return jax.shard_map(
-        per_device, mesh=mesh, in_specs=in_specs, out_specs=out_specs, check_vma=False
-    )
+        chosen, mesh=mesh, in_specs=in_specs, out_specs=out_specs, check_vma=False
+    )

time: 1270 us -> 529 us (0.42)
  waiting for transfers between devices: 655 us -> 0 us
  Pallas kernels: 0 us -> 167 us
  local copies, waits for them, and re-layouts: 283 us -> 164 us
  blocking collectives: 62.4 us -> 0 us
  matrix products: 147 us -> 125 us
  starting transfers between devices: 21.1 us -> 0 us
  between operations: 14.6 us -> 1.81 us
    reduce_scatter x1 -> x0, waiting for transfers between devices: 445 us -> none  [per_device(): lax.psum_scatter(pick_blocks(grad_blocks, slot_index, owner_slot, 1, 0),...]
    all_gather x1 -> x0, waiting for transfers between devices: 197 us -> none  [per_device(): lax.all_gather(slot_weights.astype(jnp.bfloat16), 'dp', axis=0, tiled=True)]
    pallas_call x0 -> x2, Pallas kernels: none -> 167 us  [the longest x1 95.6 us: reduce_all(): pl.pallas_call(reduce_kernel, name='reduce_all', out_shape=[jax.ShapeDtyp...]
    psum x1 -> x0, blocking collectives: 40.6 us -> none  [per_device(): vector_total = lax.psum(vector_grad, ('dp', 'sp'))]
    gather x2 -> x1, local copies, waits for them, and re-layouts: 48.8 us -> 12.4 us  [pick_blocks(): picked = jnp.take(source, chosen * fanout + part_index, axis=0)]
    all_to_all x6 -> x0, local copies, waits for them, and re-layouts: 23.2 us -> none  [the longest x2 10 us: per_device(): lax.all_to_all(projected, 'sp', split_axis=3, concat_axis=1, tiled=True)]
    all_gather x1 -> x0, blocking collectives: 21.8 us -> none  [per_device(): lax.all_gather(vector_values.astype(jnp.bfloat16), 'dp', axis=0, tiled=True)]
    mul x1 -> x0, other arithmetic: 20.7 us -> none  [pick_blocks(): return picked * present[:, None, None]]
  transfers between devices with their start and end apart: 7 -> 0, of which waited for: 4 -> 0; matrix products, arithmetic and copies ran while one was open for 8% -> 0% of each run, Pallas kernels for 0% -> 0%
where the time goes in v1:
time: 529 us; the launch traced here: 522 us
  Pallas kernels  167 us (32%)
  local copies, waits for them, and re-layouts  164 us (31%)
  matrix products  125 us (24%)
  other arithmetic  65.3 us (12%)
    pallas_call x1, Pallas kernels, reduce_all(): pl.pallas_call(reduce_kernel, name='reduce_all', out_shape=[jax.ShapeDtyp...  95.6 us
    pallas_call x1, Pallas kernels, gather_all(): pl.pallas_call(gather_kernel, name='gather_all', out_shape=[jax.ShapeDtyp...  71 us
    unnamed x167, local copies, waits for them, and re-layouts  43.8 us
    reshape x9, local copies, waits for them, and re-layouts, into_blocks(): matrix.reshape(height // BLK, BLK, breadth // BLK, BLK)  35.6 us
    dot_general x1, matrix products, fast_device(): upward = jnp.dot(hidden_half, w_upward, preferred_element_type=jnp.float32)  18.3 us
    dot_general x4, matrix products, contract_cols(): lax.dot_general(left_mat, right_mat, (((1,), (1,)), ((), ())), preferred_...  16.9 us
    reshape x6, local copies, waits for them, and re-layouts, from_blocks(): blocks.reshape(height // BLK, breadth // BLK, BLK, BLK)  14.8 us
    dot_general x4, matrix products, contract_rows(): lax.dot_general(left_mat, right_mat, (((0,), (0,)), ((), ())), preferred_...  14.8 us

profile of v1, /device:TPU:1, one launch (start us, length us, event | category | flops | bytes accessed | tf_op | source)
XLA Modules:
  0.0 522.3 jit_solution(12776259466979014018)
XLA Ops:
  15.6 71.0 %gather_all.1 = (bf16[48,400,384]{2,1,0:T(8,128)(2,1)S(1)}, bf16[4,128,768]{2,1,0:T(8,128)(2,1)S(1)}, bf16[4,128,768]{2,1,0:T(8,128)(2,1)S(1)}) custom-call(f32[6,384,384]{2,1,0:T(8,128)S(1)} %copy-done.2, f32[1,384]{1,0:T(1,128)S(1)} %reshape.339.vector, bf16[4,128,768]{2,1,0:T(8,128)(2,1)S(1)} %copy-done.8, bf16[4,128,768]{2,1,0:T(8,128)(2,1)S(1)} %copy-done.9), custom_call_target="tpu_custom_call" | custom-call | tf_op jit(solution)/shard_map/gather_all/pallas_call | solution.py:521
  86.6 5.2 copy-done.1
  96.2 12.6 %gather_fusion = bf16[48,400,384]{2,1,0:T(8,128)(2,1)} fusion(bf16[48,400,384]{2,1,0:T(8,128)(2,1)} %copy-done.1, s32[1024]{0:T(1024)S(1)} %get-tuple-element.73), kind=kCustom, calls=%fused_computation | custom fusion | bytes 29491392 | tf_op jit(solution)/shard_map/jit(_take)/gather | solution.py:823
  108.9 13.6 %broadcast_select_fusion = bf16[48,400,384]{2,1,0:T(8,128)(2,1)} fusion(bf16[48,400,384]{2,1,0:T(8,128)(2,1)} %gather_fusion, pred[48]{0:T(512)(128)(4,1)} %get-tuple-element.70), kind=kLoop, calls=%fused_computation.4 | loop fusion | flops 7372800 | bytes 29491248 | tf_op jit(solution)/shard_map/jit(_take)/select_n | solution.py:823
  131.6 8.9 %fusion.53 = (bf16[16,384,384]{2,1,0:T(8,128)(2,1)}, bf16[16,384,384]{2,1,0:T(8,128)(2,1)}) fusion(bf16[48,400,384]{2,1,0:T(8,128)(2,1)} %broadcast_select_fusion), kind=kLoop, calls=%fused_computation.146 | loop fusion | bytes 18874368 | tf_op jit(solution)/shard_map/slice | solution.py:69
  140.5 7.1 %copy.63 = bf16[8,2,384,384]{2,0,3,1:T(8,128)(2,1)} copy(bf16[8,2,384,384]{3,2,1,0:T(8,128)(2,1)} %bitcast.152) | data formatting | bytes 9437184 | tf_op jit(solution)/shard_map/reshape | solution.py:55
  147.7 5.8 %copy.95 = bf16[96,8,8,384]{3,1,2,0:T(8,128)(2,1)} copy(bf16[96,8,8,384]{3,2,1,0:T(8,128)(2,1)} %bitcast.148) | data formatting | bytes 9437184
  186.0 6.1 %fusion.26 = bf16[12,64,512]{2,1,0:T(8,128)(2,1)S(1)} fusion(bf16[512,12,64]{0,2,1:T(8,128)(2,1)} %bitcast.182, f32[12,512]{1,0:T(8,128)S(1)} %fusion, f32[12,512]{1,0:T(8,128)S(1)} %get-tuple-element.58, f32[12,512,512]{1,2,0:T(8,128)S(1)} %get-tuple-element.59, pred[512,512]{0,1:T(8,128)(4,1)} %fusion.32), kind=kOutput, calls=%fused_computation.77 | convolution fusion | flops 418775040 | bytes 14467072 | tf_op jit(solution)/shard_map/hqk,khd->qhd/dot_general | solution.py:131
  193.5 18.3 %multiply_convert_fusion.2 = (bf16[512,3072]{1,0:T(8,128)(2,1)S(1)}, f32[512,3072]{1,0:T(8,128)}, f32[512,3072]{1,0:T(8,128)}) fusion(bf16[768,3072]{1,0:T(8,128)(2,1)S(1)} %bitcast.165, f32[512,768]{1,0:T(8,128)S(1)} %get-tuple-element.61, f32[768]{0:T(1024)S(1)} %copy-done.58, f32[768]{0:T(1024)S(1)} %copy-done.51, f32[512]{0:T(512)S(1)} %fusion.35, ...), kind=kOutput, calls=%fused_computation.17 | convolution fusion | flops 2520121344 | bytes 22030336 | tf_op jit(solution)/shard_map/dot_general | solution.py:835
  217.8 7.5 %add_convert_fusion = bf16[512,3072]{1,0:T(8,128)(2,1)S(1)} fusion(f32[512,3072]{1,0:T(8,128)} %get-tuple-element.42, f32[512,3072]{1,0:T(8,128)} %get-tuple-element.62, bf16[3072,768]{0,1:T(8,128)(2,1)S(1)} %bitcast.170, f32[512,768]{1,0:T(8,128)S(1)} %get-tuple-element.40, f32[512]{0:T(512)S(1)} %negate_multiply_fusion.2), kind=kOutput, calls=%fused_computation.16 | convolution fusion | flops 2438725632 | bytes 22022144 | tf_op jit(solution)/shard_map/dot_general | solution.py:80
  234.5 10.1 %reshape.364 = bf16[8,384,2,384]{3,2,1,0:T(2,128)(2,1)} reshape(bf16[3072,768]{1,0:T(8,128)(2,1)} %convolution_convert_fusion) | data formatting | bytes 9437184 | tf_op jit(solution)/shard_map/reshape | solution.py:47
  244.6 5.5 %copy.73 = bf16[8,384,2,384]{3,1,2,0:T(8,128)(2,1)} copy(bf16[8,384,2,384]{3,2,1,0:T(2,128)(2,1)} %reshape.364) | data formatting | bytes 9437184 | tf_op jit(solution)/shard_map/reshape | solution.py:47
  252.1 5.0 convolution_convert_fusion.1
  274.5 8.9 %fusion.3 = bf16[12,64,512]{2,1,0:T(8,128)(2,1)} fusion(bf16[512,12,64]{0,2,1:T(8,128)(2,1)} %bitcast.184, f32[12,512]{1,0:T(8,128)} %log_add_fusion, f32[12,512,512]{1,2,0:T(8,128)} %copy-done.14, pred[512,512]{0,1:T(8,128)(4,1)} %fusion.32), kind=kOutput, calls=%fused_computation.15 | convolution fusion | flops 415236096 | bytes 14442496 | tf_op jit(solution)/shard_map/hqk,qhd->khd/dot_general | solution.py:143
  290.2 11.0 %multiply_reduce_fusion = (f32[12,512]{1,0:T(8,128)S(1)}, f32[12,512,512]{1,2,0:T(8,128)}) fusion(f32[12,512]{1,0:T(8,128)} %log_add_fusion, f32[12,512,512]{1,2,0:T(8,128)} %copy-done.14, pred[512,512]{0,1:T(8,128)(4,1)} %fusion.32, bf16[512,12,64]{0,2,1:T(8,128)(2,1)S(1)} %bitcast.185, bf16[512,12,64]{0,2,1:T(8,128)(2,1)S(1)} %bitcast.183), kind=kOutput, calls=%fused_computation.6 | convolution fusion | flops 418375680 | bytes 27049984 | tf_op jit(solution)/shard_map/qhd,khd->hqk/dot_general | solution.py:146
  302.9 7.5 %multiply_convert_fusion.1 = bf16[12,512,512]{1,2,0:T(8,128)(2,1)S(1)} fusion(f32[12,512,512]{1,2,0:T(8,128)} %get-tuple-element.67, f32[12,512]{1,0:T(8,128)S(1)} %get-tuple-element.66, f32[12,512]{1,0:T(8,128)S(1)} %copy-done.50, f32[12,512,512]{1,2,0:T(8,128)S(1)} %bitcast.143, pred[512,512]{0,1:T(8,128)(4,1)S(1)} %copy-done.21), kind=kLoop, calls=%fused_computation.5 | loop fusion | flops 18874368 | bytes 31768576 | tf_op jit(solution)/shard_map/convert_element_type | solution.py:148
  344.2 5.6 %constant_dynamic-update-slice_fusion.4 = bf16[48,384,384]{2,1,0:T(8,128)(2,1)} fusion(bf16[48,384,384]{2,1,0:T(8,128)(2,1)} %constant_dynamic-update-slice_fusion.5, bf16[16,384,384]{2,1,0:T(8,128)(2,1)} %bitcast.147), kind=kLoop, calls=%fused_computation.94 | loop fusion | bytes 9437184
  352.5 12.4 %gather_fusion.1 = bf16[48,384,384]{2,1,0:T(8,128)(2,1)} fusion(bf16[48,384,384]{2,1,0:T(8,128)(2,1)} %constant_dynamic-update-slice_fusion.3, s32[1024]{0:T(1024)} %get-tuple-element.72), kind=kCustom, calls=%fused_computation.1 | custom fusion | bytes 28311744 | tf_op jit(solution)/shard_map/jit(_take)/gather | solution.py:173
  364.9 14.3 %multiply_convert_fusion = bf16[48,384,384]{2,1,0:T(8,128)(2,1)} fusion(f32[48]{0:T(128)S(1)} %copy-done.63, bf16[48,384,384]{2,1,0:T(8,128)(2,1)} %gather_fusion.1, pred[48]{0:T(512)(128)(4,1)S(1)} %copy-done.60), kind=kLoop, calls=%fused_computation.2 | loop fusion | flops 28311552 | bytes 28311792 | tf_op jit(solution)/shard_map/convert_element_type | solution.py:869
  379.2 8.1 %pad_maximum_fusion.grads = bf16[48,400,384]{2,1,0:T(8,128)(2,1)S(1)} fusion(bf16[48,16,384]{2,1,0:T(8,128)(2,1)S(1)} %copy-done.42, bf16[48,384,384]{2,1,0:T(8,128)(2,1)} %multiply_convert_fusion), kind=kLoop, calls=%fused_computation.3 | loop fusion | flops 29491200 | bytes 29491200 | tf_op jit(solution)/shard_map/concatenate | solution.py:873
  387.4 95.6 %reduce_all.1 = (bf16[6,400,384]{2,1,0:T(8,128)(2,1)S(1)}, bf16[4,128,768]{2,1,0:T(8,128)(2,1)S(1)}, bf16[4,128,768]{2,1,0:T(8,128)(2,1)S(1)}) custom-call(bf16[48,400,384]{2,1,0:T(8,128)(2,1)S(1)} %pad_maximum_fusion.grads, bf16[4,128,768]{2,1,0:T(8,128)(2,1)S(1)} %bitcast.137, bf16[4,128,768]{2,1,0:T(8,128)(2,1)S(1)} %bitcast.138), custom_call_target="tpu_custom_call" | custom-call | tf_op jit(solution)/shard_map/reduce_all/pallas_call | solution.py:782
  495.1 8.1 %fusion.13 = (f32[6,384,384]{2,1,0:T(8,128)S(1)}, f32[6,384,384]{2,1,0:T(8,128)S(1)}) fusion(f32[6,384,384]{2,1,0:T(8,128)S(1)} %copy-done.36, f32[6,384,384]{2,1,0:T(8,128)S(1)} %copy-done.37, f32[6,384,384]{1,2,0:T(8,128)S(1)} %fusion.29, f32[6,384,384]{2,1,0:T(8,128)S(1)} %copy-done), kind=kOutput, calls=%fused_computation.41 | convolution fusion | flops 4082171904 | bytes 21233664 | tf_op jit(solution)/shard_map/nij,njk->nik/dot_general | solution.py:95
  503.2 8.7 %fusion.14 = f32[6,384,384]{1,2,0:T(8,128)S(1)} fusion(f32[6,384,384]{2,1,0:T(8,128)S(1)} %copy-done.35, f32[6,384,384]{2,1,0:T(8,128)S(1)} %get-tuple-element.88, f32[6,384,384]{2,1,0:T(8,128)S(1)} %get-tuple-element.87), kind=kOutput, calls=%fused_computation.43 | convolution fusion | flops 4080402432 | bytes 14155776 | tf_op jit(solution)/shard_map/nij,njk->nik/dot_general | solution.py:100
  512.0 9.2 %fusion.59 = (bf16[6,384,384]{2,1,0:T(8,128)(2,1)}, f32[6,384,384]{2,1,0:T(8,128)}) fusion(f32[6,384,384]{2,1,0:T(8,128)S(1)} %copy-done.3, f32[6,384,384]{1,2,0:T(8,128)S(1)} %fusion.14, f32[6,384,384]{2,1,0:T(8,128)S(1)} %copy-done), kind=kOutput, calls=%fused_computation.152 | convolution fusion | flops 4079517696 | bytes 15925248 | tf_op jit(solution)/shard_map/nij,nkj->nik/dot_general | solution.py:101
  (254 shorter events, 154.5 us)
Async XLA Ops:
  0.6 494.4 %copy-start = (f32[6,384,384]{2,1,0:T(8,128)S(1)}, f32[6,384,384]{2,1,0:T(8,128)}, u32[]{:S(2)}) copy-start(f32[6,384,384]{2,1,0:T(8,128)} %param.26) | copy-start | bytes 10616836
  185.1 8.3 %slice-start.5 = ((s8[4718592]{0:T(1024)(128)(4,1)}), s8[4194304]{0:T(1024)(128)(4,1)S(1)}, s32[]{:S(2)}) async-start(s8[4718592]{0:T(1024)(128)(4,1)} %bitcast.163), calls=%async_computation.5 | async-start | bytes 8388608
  192.1 19.6 %copy-start.64 = (bf16[12,64,512]{2,1,0:T(8,128)(2,1)}, bf16[12,64,512]{2,1,0:T(8,128)(2,1)S(1)}, u32[]{:S(2)}) copy-start(bf16[12,64,512]{2,1,0:T(8,128)(2,1)S(1)} %fusion.26) | copy-start | bytes 2359300
  192.2 19.6 %slice-start.7 = ((s8[4718592]{0:T(1024)(128)(4,1)}), s8[4194304]{0:T(1024)(128)(4,1)S(1)}, s32[]{:S(2)}) async-start(s8[4718592]{0:T(1024)(128)(4,1)} %bitcast.167), calls=%async_computation.7 | async-start | bytes 8388608
  193.1 32.3 %copy-start.22 = (f32[512,768]{1,0:T(8,128)}, f32[512,768]{1,0:T(8,128)S(1)}, u32[]{:S(2)}) copy-start(f32[512,768]{1,0:T(8,128)S(1)} %get-tuple-element.61) | copy-start | bytes 4718596
  193.5 31.9 %copy-start.54 = (f32[512]{0:T(512)}, f32[512]{0:T(512)S(1)}, u32[]{:S(2)}) copy-start(f32[512]{0:T(512)S(1)} %fusion.35) | copy-start | bytes 6148
  193.5 18.3 %slice-start.8 = ((s8[4718592]{0:T(1024)(128)(4,1)}), s8[524288]{0:T(1024)(128)(4,1)S(1)}, s32[]{:S(2)}) async-start(s8[4718592]{0:T(1024)(128)(4,1)} %bitcast.167), calls=%async_computation.8 | async-start | bytes 1048576
  274.5 8.9 %copy-start.25 = (f32[512,768]{1,0:T(8,128)S(1)}, f32[512,768]{1,0:T(8,128)}, u32[]{:S(2)}) copy-start(f32[512,768]{1,0:T(8,128)} %copy-done.24) | copy-start | bytes 4718596
  290.1 11.1 %slice-start = ((s8[12582912]{0:T(1024)(128)(4,1)}), s8[4194304]{0:T(1024)(128)(4,1)S(1)}, s32[]{:S(2)}) async-start(s8[12582912]{0:T(1024)(128)(4,1)} %bitcast.142), calls=%async_computation | async-start | bytes 8388608
  290.1 11.1 %slice-start.1 = ((s8[12582912]{0:T(1024)(128)(4,1)}), s8[4194304]{0:T(1024)(128)(4,1)S(1)}, s32[]{:S(2)}) async-start(s8[12582912]{0:T(1024)(128)(4,1)} %bitcast.142), calls=%async_computation.1 | async-start | bytes 8388608
  290.1 12.8 %slice-start.2 = ((s8[12582912]{0:T(1024)(128)(4,1)}), s8[4194304]{0:T(1024)(128)(4,1)S(1)}, s32[]{:S(2)}) async-start(s8[12582912]{0:T(1024)(128)(4,1)} %bitcast.142), calls=%async_computation.2 | async-start | bytes 8388608
  290.1 12.8 %copy-start.21 = (pred[512,512]{0,1:T(8,128)(4,1)S(1)}, pred[512,512]{0,1:T(8,128)(4,1)}, u32[]{:S(2)}) copy-start(pred[512,512]{0,1:T(8,128)(4,1)} %fusion.32) | copy-start | bytes 786436
  290.2 12.8 %copy-start.50 = (f32[12,512]{1,0:T(8,128)S(1)}, f32[12,512]{1,0:T(8,128)}, u32[]{:S(2)}) copy-start(f32[12,512]{1,0:T(8,128)} %log_add_fusion) | copy-start | bytes 73732
  352.5 12.4 %copy-start.60 = (pred[48]{0:T(512)(128)(4,1)S(1)}, pred[48]{0:T(512)(128)(4,1)}, u32[]{:S(2)}) copy-start(pred[48]{0:T(512)(128)(4,1)} %get-tuple-element.71) | copy-start | bytes 148
  352.5 12.4 %copy-start.63 = (f32[48]{0:T(128)S(1)}, f32[48]{0:T(128)}, u32[]{:S(2)}) copy-start(f32[48]{0:T(128)} %convert_element_type.132) | copy-start | bytes 580
  364.9 14.3 %copy-start.42 = (bf16[48,16,384]{2,1,0:T(8,128)(2,1)S(1)}, bf16[48,16,384]{2,1,0:T(8,128)(2,1)}, u32[]{:S(2)}) copy-start(bf16[48,16,384]{2,1,0:T(8,128)(2,1)} %broadcast_in_dim.101) | copy-start | bytes 1769476
  379.2 8.1 %copy-start.7 = (bf16[512,768]{1,0:T(8,128)(2,1)S(1)}, bf16[512,768]{1,0:T(8,128)(2,1)}, u32[]{:S(2)}) copy-start(bf16[512,768]{1,0:T(8,128)(2,1)} %add_convert_fusion.1) | copy-start | bytes 2359300
  387.3 95.7 %copy-start.56 = (f32[384]{0:T(512)S(1)}, f32[384]{0:T(512)}, u32[]{:S(2)}) copy-start(f32[384]{0:T(512)} %param.27) | copy-start | bytes 4612
  387.3 95.7 %copy-start.61 = (f32[384]{0:T(512)S(1)}, f32[384]{0:T(512)}, u32[]{:S(2)}) copy-start(f32[384]{0:T(512)} %param.29) | copy-start | bytes 4612
  387.4 95.7 %copy-start.62 = (f32[384]{0:T(512)S(1)}, f32[384]{0:T(512)}, u32[]{:S(2)}) copy-start(f32[384]{0:T(512)} %param.28) | copy-start | bytes 4612
  387.4 97.6 %copy-start.33 = (f32[6,384,384]{2,1,0:T(8,128)S(1)}, f32[6,384,384]{2,1,0:T(8,128)}, u32[]{:S(2)}) copy-start(f32[6,384,384]{2,1,0:T(8,128)} %param.23) | copy-start | bytes 10616836
  503.2 8.8 %copy-start.38 = (f32[6,384,384]{2,1,0:T(8,128)}, f32[6,384,384]{2,1,0:T(8,128)S(1)}, u32[]{:S(2)}) copy-start(f32[6,384,384]{2,1,0:T(8,128)S(1)} %get-tuple-element.88) | copy-start | bytes 10616836
  503.2 8.8 %copy-start.39 = (f32[6,384,384]{2,1,0:T(8,128)}, f32[6,384,384]{2,1,0:T(8,128)S(1)}, u32[]{:S(2)}) copy-start(f32[6,384,384]{2,1,0:T(8,128)S(1)} %get-tuple-element.87) | copy-start | bytes 10616836
  503.2 8.8 %copy-start.3 = (f32[6,384,384]{2,1,0:T(8,128)S(1)}, f32[6,384,384]{2,1,0:T(8,128)}, u32[]{:S(2)}) copy-start(f32[6,384,384]{2,1,0:T(8,128)} %weights.1) | copy-start | bytes 10616836
  (52 other events, 187.2 us)

commit v2 on v1

--- a/solution.py
+++ b/solution.py
@@ -1,4 +1,5 @@
-import functools
+import math
+
 import jax
 import jax.numpy as jnp
 from jax import lax
@@ -306,6 +307,10 @@
 NZ = 4
 
 
+def in_hbm(value):
+    return pltpu.with_memory_space_constraint(value, pltpu.HBM)
+
+
 def place():
     dp = lax.axis_index("dp")
     sp = lax.axis_index("sp")
@@ -517,14 +522,14 @@
 
 
 def gather_all(weights, vector, tokens, grads):
-    anywhere = pl.BlockSpec(memory_space=pl.ANY)
+    anywhere = pl.BlockSpec(memory_space=pltpu.HBM)
     return pl.pallas_call(
         gather_kernel,
         name="gather_all",
         out_shape=[
-            jax.ShapeDtypeStruct((48, PITCH, BLK), jnp.bfloat16),
-            jax.ShapeDtypeStruct(tokens.shape, jnp.bfloat16),
-            jax.ShapeDtypeStruct(grads.shape, jnp.bfloat16),
+            pltpu.HBM((48, PITCH, BLK), jnp.bfloat16),
+            pltpu.HBM(tokens.shape, jnp.bfloat16),
+            pltpu.HBM(grads.shape, jnp.bfloat16),
         ],
         in_specs=[anywhere, pl.BlockSpec(memory_space=pltpu.VMEM), anywhere, anywhere],
         out_specs=[anywhere, anywhere, anywhere],
@@ -542,7 +547,348 @@
         compiler_params=pltpu.CompilerParams(
             collective_id=0, has_side_effects=True, vmem_limit_bytes=24 << 20
         ),
-    )(weights, vector.reshape(1, BLK), tokens, grads)
+    )(in_hbm(weights), vector.reshape(1, BLK), in_hbm(tokens), in_hbm(grads))
+
+
+ROW = 512
+PAIR = 128
+SPAN = 384
+EPS = 1e-06
+
+
+def erf_of(x):
+    x = jnp.clip(x, -3.832506856900711, 3.832506856900711)
+    s = x * x
+    top = 0.00022905065861350646
+    for term in (0.0034082910107109506, 0.050955695062380861, 0.18520832239976145, 1.128379143519084):
+        top = top * s + term
+    bottom = -1.1791602954361697e-7
+    for term in (0.000023547966471313185, 0.0010179625278914885, 0.014070470171167667,
+                 0.11098505178285362, 0.49746925110067538, 1.0):
+        bottom = bottom * s + term
+    return x * top / bottom
+
+
+def dot_nn(a, b):
+    return lax.dot_general(a, b, (((1,), (0,)), ((), ())), preferred_element_type=jnp.float32)
+
+
+def dot_nt(a, b):
+    return lax.dot_general(a, b, (((1,), (1,)), ((), ())), preferred_element_type=jnp.float32)
+
+
+def dot_tn(a, b):
+    return lax.dot_general(a, b, (((0,), (0,)), ((), ())), preferred_element_type=jnp.float32)
+
+
+def layer_kernel(
+    owner, weights, tokens, dy_ref, segments, grads, block_out, input_half,
+    wqkv, wo, w1, w2, gains, qkv, probs, context, hidden, hidden16, norm1, act, slope, acc, dz, dz16,
+    dqkv, dup, stage, vecs, spread, w_sem, g_sem, v_sem,
+):
+    half = jnp.bfloat16
+    sp = lax.axis_index("sp")
+
+    def weight_copies():
+        copies = []
+        for which, ref in enumerate((wqkv.at[0], wqkv.at[1], wqkv.at[2], wo)):
+            for r in range(2):
+                for q in range(2):
+                    copies.append((which * 4 + r * 2 + q, ref, r, q))
+        for r in range(2):
+            for q in range(8):
+                copies.append((16 + r * 8 + q, w1.at[q // 2], r, q % 2))
+        for r in range(8):
+            for q in range(2):
+                copies.append((32 + r * 2 + q, w2.at[r // 2], r % 2, q))
+        return [
+            pltpu.make_async_copy(
+                weights.at[owner[b], pl.ds(0, BLK)],
+                ref.at[pl.ds(r * BLK, BLK), pl.ds(q * BLK, BLK)],
+                w_sem.at[b],
+            )
+            for b, ref, r, q in copies
+        ]
+
+    copies = weight_copies()
+    gain_copies = [
+        pltpu.make_async_copy(
+            weights.at[6 * d, pl.ds(BLK, 16)], gains.at[d // 2, :, pl.ds((d % 2) * BLK, BLK)], g_sem.at[d]
+        )
+        for d in range(8)
+    ]
+    for item in copies[:16] + gain_copies + copies[16:]:
+        item.start()
+
+    seg_row = segments[pl.ds(sp, 1), :].astype(jnp.float32)
+    spread[...] = jnp.transpose(jnp.broadcast_to(seg_row, (PAIR, ROW)))
+
+    for item in copies[:12]:
+        item.wait()
+    x = tokens[...]
+    for part in range(3):
+        block = dot_nn(x, wqkv[part])
+        if part == 0:
+            block = block * 0.125
+        block = block.astype(half)
+        for p in range(6):
+            qkv[part * 6 + p] = block[:, p * PAIR : (p + 1) * PAIR]
+
+    lane = lax.broadcasted_iota(jnp.int32, (1, PAIR), 1)
+    lows = (lane < 64, lane >= 64)
+
+    def visible(part):
+        keys = segments[pl.ds(sp, 1), pl.ds(part * PAIR, SPAN)].astype(jnp.float32)
+        own = spread[pl.ds(part * 256, 256), pl.ds(0, 1)]
+        return own == keys
+
+    def attend(p, carry):
+        q2, k2, v2 = qkv[p], qkv[6 + p], qkv[12 + p]
+        for part in range(2):
+            mask = visible(part)
+            qs = q2[part * 256 : part * 256 + 256]
+            ks = k2[part * PAIR : part * PAIR + SPAN]
+            vs = v2[part * PAIR : part * PAIR + SPAN]
+            outs = []
+            for h in range(2):
+                scores = dot_nt(jnp.where(lows[h], qs, jnp.zeros_like(qs)), ks)
+                scores = jnp.where(mask, scores, -1e30)
+                top = jnp.max(scores, axis=1, keepdims=True)
+                raised = jnp.exp(scores - top)
+                prob = raised * (1.0 / jnp.sum(raised, axis=1, keepdims=True))
+                probs[p, 2 * part + h] = prob
+                outs.append(dot_nn(prob.astype(half), vs))
+            context[p, pl.ds(part * 256, 256)] = jnp.where(lows[0], outs[0], outs[1]).astype(half)
+        return carry
+
+    lax.fori_loop(0, 6, attend, 0)
+
+    for item in copies[12:16] + gain_copies:
+        item.wait()
+    joined = jnp.concatenate([context[p] for p in range(6)], axis=1)
+
+    def gain(k):
+        return gains[k, pl.ds(0, 1), :].astype(jnp.float32)
+
+    def normalise(z):
+        centre = jnp.mean(z, axis=1, keepdims=True)
+        z = z - centre
+        inverse = lax.rsqrt(jnp.mean(z * z, axis=1, keepdims=True) + EPS)
+        return z * inverse, inverse
+
+    acc[...] = dot_nn(joined, wo[...])
+
+    def norm_one(t, carry):
+        rows = pl.ds(pl.multiple_of(t * 64, 64), 64)
+        hat, inverse = normalise(tokens[rows, :].astype(jnp.float32) + acc[rows, :])
+        norm1[rows, :] = hat
+        spread[rows, :] = jnp.where(lane == 1, inverse, spread[rows, :])
+        value = hat * gain(0) + gain(1)
+        hidden[rows, :] = value
+        hidden16[rows, :] = value.astype(half)
+        return carry
+
+    lax.fori_loop(0, 8, norm_one, 0)
+    for item in copies[16:]:
+        item.wait()
+
+    def forward(j, carry):
+        up = dot_nn(hidden16[...], w1[j])
+        phi_big = 0.5 + 0.5 * erf_of(up * (1.0 / math.sqrt(2.0)))
+        value = (up * phi_big).astype(half)
+        slope[j] = phi_big + up * (jnp.exp(-0.5 * up * up) * (1.0 / math.sqrt(2.0 * math.pi)))
+        act[j] = value
+        part = dot_nn(value, w2[j])
+        hidden[...] += part
+        return carry
+
+    lax.fori_loop(0, 4, forward, 0)
+
+    vecs[...] = jnp.zeros_like(vecs)
+
+    def fold(value):
+        return jnp.sum(value.reshape(-1, 8, D), axis=0)
+
+    def norm_back(hat, inverse, delta, gain_row):
+        e = delta * gain_row
+        return (
+            e - jnp.mean(e, axis=1, keepdims=True) - hat * jnp.mean(e * hat, axis=1, keepdims=True)
+        ) * inverse
+
+    def norm_two(t, carry):
+        rows = pl.ds(pl.multiple_of(t * 64, 64), 64)
+        hat, inverse = normalise(hidden[rows, :])
+        block_out[rows, :] = (hat * gain(2) + gain(3)).astype(half)
+        delta = dy_ref[rows, :].astype(jnp.float32)
+        vecs[2] += fold(delta * hat)
+        vecs[3] += fold(delta)
+        back = norm_back(hat, inverse, delta, gain(2))
+        dz[rows, :] = back
+        dz16[rows, :] = back.astype(half)
+        return carry
+
+    lax.fori_loop(0, 8, norm_two, 0)
+
+    def out_copy(slot, b, r, q):
+        return pltpu.make_async_copy(
+            stage.at[slot, pl.ds(r * BLK, BLK), pl.ds(q * BLK, BLK)],
+            grads.at[owner[b], pl.ds(0, BLK)],
+            v_sem.at[slot, r * 2 + q],
+        )
+
+    def flush(slot, blocks):
+        for r in range(2):
+            for q in range(2):
+                out_copy(slot, blocks(r, q), r, q).start()
+
+    def drain(slot):
+        for r in range(2):
+            for q in range(2):
+                out_copy(slot, 0, r, q).wait()
+
+    def backward(j, carry):
+        ddown = dz16[...]
+        delta = (dot_nt(ddown, w2[j]) * slope[j]).astype(half)
+
+        @pl.when(j >= 2)
+        def _():
+            drain(2 * (j % 2))
+            drain(2 * (j % 2) + 1)
+
+        stage[2 * (j % 2)] = dot_tn(act[j], ddown).astype(half)
+        flush(2 * (j % 2), lambda r, q: 32 + (2 * j + r) * 2 + q)
+        stage[2 * (j % 2) + 1] = dot_tn(hidden16[...], delta).astype(half)
+        flush(2 * (j % 2) + 1, lambda r, q: 16 + r * 8 + 2 * j + q)
+        dz[...] += dot_nt(delta, w1[j])
+        return carry
+
+    lax.fori_loop(0, 4, backward, 0)
+
+    def norm_one_back(t, carry):
+        rows = pl.ds(pl.multiple_of(t * 64, 64), 64)
+        hat = norm1[rows, :]
+        delta = dz[rows, :]
+        vecs[0] += fold(delta * hat)
+        vecs[1] += fold(delta)
+        back = norm_back(hat, spread[rows, pl.ds(1, 1)], delta, gain(0))
+        dz[rows, :] = back
+        dz16[rows, :] = back.astype(half)
+        return carry
+
+    lax.fori_loop(0, 8, norm_one_back, 0)
+
+    for slot in range(4):
+        drain(slot)
+    dattn = dz16[...]
+    stage[0] = dot_tn(joined, dattn).astype(half)
+    flush(0, lambda r, q: 12 + r * 2 + q)
+    dcontext = dot_nt(dattn, wo[...]).astype(half)
+    for p in range(6):
+        context[p] = dcontext[:, p * PAIR : (p + 1) * PAIR]
+
+    def attend_back(p, carry):
+        q2, k2, v2, d2 = qkv[p], qkv[6 + p], qkv[12 + p], context[p]
+        dup[...] = jnp.zeros_like(dup)
+        for part in range(2):
+            window = pl.ds(part * PAIR, SPAN)
+            qs = q2[part * 256 : part * 256 + 256]
+            ds = d2[part * 256 : part * 256 + 256]
+            ks = k2[part * PAIR : part * PAIR + SPAN]
+            vs = v2[part * PAIR : part * PAIR + SPAN]
+            dvs, dqs, dks = [], [], []
+            for h in range(2):
+                prob = probs[p, 2 * part + h]
+                dprob = dot_nt(jnp.where(lows[h], ds, jnp.zeros_like(ds)), vs)
+                product = prob * dprob
+                dscore = (product - prob * jnp.sum(product, axis=1, keepdims=True)).astype(half)
+                dvs.append(dot_tn(prob.astype(half), ds))
+                dqs.append(dot_nn(dscore, ks))
+                dks.append(dot_tn(dscore, qs))
+            dqkv[p, pl.ds(part * 256, 256)] = (
+                jnp.where(lows[0], dqs[0], dqs[1]) * 0.125
+            ).astype(half)
+            dup[0, window] += jnp.where(lows[0], dks[0], dks[1])
+            dup[1, window] += jnp.where(lows[0], dvs[0], dvs[1])
+        dqkv[6 + p] = dup[0].astype(half)
+        dqkv[12 + p] = dup[1].astype(half)
+        return carry
+
+    lax.fori_loop(0, 6, attend_back, 0)
+
+    for part in range(3):
+        delta = jnp.concatenate([dqkv[part * 6 + p] for p in range(6)], axis=1)
+        stage[1 + part] = dot_tn(x, delta).astype(half)
+        flush(1 + part, lambda r, q: part * 4 + r * 2 + q)
+        dz[...] += dot_nt(delta, wqkv[part])
+
+    input_half[...] = dz[...].astype(half)
+    for k in range(4):
+        row = jnp.sum(vecs[k], axis=0, keepdims=True)
+        vecs16 = jnp.broadcast_to(row, (16, D)).astype(half)
+        gains[k] = vecs16
+    for k in range(4):
+        for q in range(2):
+            for s in range(2):
+                pltpu.make_async_copy(
+                    gains.at[k, :, pl.ds(q * BLK, BLK)],
+                    grads.at[6 * (2 * k + q) + s, pl.ds(BLK, 16)],
+                    w_sem.at[(2 * k + q) * 2 + s],
+                ).start()
+    for k in range(4):
+        for q in range(2):
+            for s in range(2):
+                pltpu.make_async_copy(
+                    gains.at[k, :, pl.ds(q * BLK, BLK)],
+                    grads.at[6 * (2 * k + q) + s, pl.ds(BLK, 16)],
+                    w_sem.at[(2 * k + q) * 2 + s],
+                ).wait()
+    for slot in range(4):
+        drain(slot)
+
+
+def run_layer(owner_slot, gathered, token_row, grad_row, segment_ids):
+    half, full = jnp.bfloat16, jnp.float32
+    anywhere = pl.BlockSpec(memory_space=pltpu.HBM)
+    vmem = pl.BlockSpec(memory_space=pltpu.VMEM)
+    dma = pltpu.SemaphoreType.DMA
+    return pl.pallas_call(
+        layer_kernel,
+        name="run_layer",
+        out_shape=[
+            jax.ShapeDtypeStruct((48, PITCH, BLK), half),
+            jax.ShapeDtypeStruct((ROW, D), half),
+            jax.ShapeDtypeStruct((ROW, D), half),
+        ],
+        in_specs=[pl.BlockSpec(memory_space=pltpu.SMEM), anywhere, vmem, vmem, vmem],
+        out_specs=[anywhere, vmem, vmem],
+        scratch_shapes=[
+            pltpu.VMEM((3, D, D), half),
+            pltpu.VMEM((D, D), half),
+            pltpu.VMEM((4, D, D), half),
+            pltpu.VMEM((4, D, D), half),
+            pltpu.VMEM((4, 16, D), half),
+            pltpu.VMEM((18, ROW, PAIR), half),
+            pltpu.VMEM((6, 4, 256, SPAN), full),
+            pltpu.VMEM((6, ROW, PAIR), half),
+            pltpu.VMEM((ROW, D), full),
+            pltpu.VMEM((ROW, D), half),
+            pltpu.VMEM((ROW, D), full),
+            pltpu.VMEM((4, ROW, D), half),
+            pltpu.VMEM((4, ROW, D), full),
+            pltpu.VMEM((ROW, D), full),
+            pltpu.VMEM((ROW, D), full),
+            pltpu.VMEM((ROW, D), half),
+            pltpu.VMEM((18, ROW, PAIR), half),
+            pltpu.VMEM((2, ROW, PAIR), full),
+            pltpu.VMEM((4, D, D), half),
+            pltpu.VMEM((4, 8, D), full),
+            pltpu.VMEM((ROW, PAIR), full),
+            dma((48,)),
+            dma((8,)),
+            dma((4, 4)),
+        ],
+        compiler_params=pltpu.CompilerParams(vmem_limit_bytes=62 << 20),
+    )(owner_slot, gathered, token_row, grad_row, segment_ids)
 
 
 BLANK = BLK + 16
@@ -775,7 +1121,7 @@
 
 
 def reduce_all(grads, rows_a, rows_b):
-    anywhere = pl.BlockSpec(memory_space=pl.ANY)
+    anywhere = pl.BlockSpec(memory_space=pltpu.HBM)
     half = jnp.bfloat16
     heights = (BLANK, BLK, HALF, HALF)
     dma = pltpu.SemaphoreType.DMA
@@ -784,8 +1130,8 @@
         name="reduce_all",
         out_shape=[
             jax.ShapeDtypeStruct((6, PITCH, BLK), half),
-            jax.ShapeDtypeStruct(rows_a.shape, half),
-            jax.ShapeDtypeStruct(rows_b.shape, half),
+            pltpu.HBM(rows_a.shape, half),
+            pltpu.HBM(rows_b.shape, half),
         ],
         in_specs=[anywhere] * 3,
         out_specs=[anywhere] * 3,
@@ -803,86 +1149,85 @@
         compiler_params=pltpu.CompilerParams(
             collective_id=1, has_side_effects=True, vmem_limit_bytes=30 << 20
         ),
-    )(grads, rows_a, rows_b)
-
-
-def attend_dense(joint, segment_row, length_row):
-    return attend_rows((joint, segment_row, length_row))
+    )(in_hbm(grads), in_hbm(rows_a), in_hbm(rows_b))
+
+
+CORRECT = 1.0 - 0.5**STEP
+
+
+def update_kernel(
+    total, weights, first, second, left, right, left_rot, right_rot, vec_grad, vec, vec_first, vec_second,
+    moment_one, moment_two, left_new, right_new, weights_new, weights_half, vector_one, vector_two, vector_new,
+):
+    half = jnp.bfloat16
+    grad = total[0, :BLK, :]
+    left_new[0] = 0.95 * left[0] + 0.05 * dot_nt(grad, grad)
+    right_new[0] = 0.95 * right[0] + 0.05 * dot_tn(grad, grad)
+    rot_l = left_rot[0].astype(half)
+    rot_r = right_rot[0].astype(half)
+    turned = dot_nn(dot_tn(rot_l, grad).astype(half), rot_r)
+    one = 0.5 * first[0] + 0.5 * turned
+    two = 0.5 * second[0] + 0.5 * turned * turned
+    moment_one[0] = one
+    moment_two[0] = two
+    ratio = (one / CORRECT) / (jnp.sqrt(two / CORRECT) + 1e-08)
+    stepped = dot_nt(dot_nn(rot_l, ratio.astype(half)).astype(half), rot_r)
+    fresh = weights[0] - rate_matrix * stepped
+    weights_new[0] = fresh
+    weights_half[0] = fresh.astype(half)
+
+    @pl.when(pl.program_id(0) == 0)
+    def _():
+        slope = vec_grad[0, :1, :].astype(jnp.float32)
+        vec_one = 0.5 * vec_first[...] + 0.5 * slope
+        vec_two = 0.5 * vec_second[...] + 0.5 * slope * slope
+        vector_one[...] = vec_one
+        vector_two[...] = vec_two
+        vector_new[...] = vec[...] - rate_vector * (
+            (vec_one / CORRECT) / (jnp.sqrt(vec_two / CORRECT) + 1e-08)
+        )
+
+
+def update_all(total, weights, first, second, left, right, left_rot, right_rot, vec, vec_first, vec_second):
+    full = jnp.float32
+    holding = weights.shape[0]
+    block = pl.BlockSpec((1, BLK, BLK), lambda i: (i, 0, 0))
+    row = pl.BlockSpec((1, BLK), lambda i: (0, 0))
+    vector = jax.ShapeDtypeStruct((1, BLK), full)
+    matrix = jax.ShapeDtypeStruct(weights.shape, full)
+    return pl.pallas_call(
+        update_kernel,
+        name="update_all",
+        grid=(holding,),
+        out_shape=[matrix] * 5 + [jax.ShapeDtypeStruct(weights.shape, jnp.bfloat16)] + [vector] * 3,
+        in_specs=[pl.BlockSpec((1, PITCH, BLK), lambda i: (i, 0, 0))]
+        + [block] * 7
+        + [pl.BlockSpec((1, 16, BLK), lambda i: (0, BLK // 16, 0)), row, row, row],
+        out_specs=[block] * 6 + [row] * 3,
+        compiler_params=pltpu.CompilerParams(vmem_limit_bytes=30 << 20),
+    )(
+        total, weights, first, second, left, right, left_rot, right_rot, total,
+        vec.reshape(1, BLK), vec_first.reshape(1, BLK), vec_second.reshape(1, BLK),
+    )
 
 
 def fast_device(
     tokens, output_grad, segment_ids, lengths, owner_slot, slot_weights, first_moment, second_moment,
     left_stats, right_stats, left_basis, right_basis, vector_values, vector_first, vector_second,
 ):
-    row_count, token_count = tokens.shape[0], tokens.shape[1]
-    place_sp = lax.axis_index("sp")
     gathered, token_row, grad_row = gather_all(slot_weights, vector_values, tokens, output_grad)
-    gains = gathered[::6, BLK].reshape(4, D).astype(jnp.float32)
-    segment_row = lax.dynamic_index_in_dim(segment_ids, place_sp, 0, False)
-    length_row = lax.dynamic_index_in_dim(lengths, place_sp, 0, False)
-    blocks = jnp.take(gathered, owner_slot, axis=0)[:, :BLK]
-    w_query, w_key, w_value, w_output, w_upward, w_downward = split_blocks(blocks)
-    w_joint = jnp.concatenate([w_query, w_key, w_value], axis=1)
-    flat_tokens = token_row.reshape(-1, D)
-    count = flat_tokens.shape[0]
-    projected = jnp.dot(flat_tokens, w_joint, preferred_element_type=jnp.float32).astype(jnp.bfloat16)
-    joint = projected.reshape(count, 3, D)
-    context_tok, logsum = attend_rows((joint, segment_row, length_row))
-    attended = jnp.dot(context_tok, w_output, preferred_element_type=jnp.float32)
-    summed_one = flat_tokens.astype(jnp.float32) + attended
-    hidden, norm_one_pull = jax.vjp(layer_norm, summed_one, gains[0], gains[1])
-    hidden_half = hidden.astype(jnp.bfloat16)
-    upward = jnp.dot(hidden_half, w_upward, preferred_element_type=jnp.float32)
-    activated, gelu_pull = jax.vjp(exact_gelu, upward)
-    active_half = activated.astype(jnp.bfloat16)
-    downward = jnp.dot(active_half, w_downward, preferred_element_type=jnp.float32)
-    result, norm_two_pull = jax.vjp(layer_norm, hidden + downward, gains[2], gains[3])
-    block_row = result.astype(jnp.bfloat16)
-    cotangent = grad_row.reshape(-1, D).astype(jnp.float32)
-    delta_two, delta_gain_two, delta_shift_two = norm_two_pull(cotangent)
-    delta_down = delta_two.astype(jnp.bfloat16)
-    grad_down = contract_rows(active_half, delta_down)
-    (delta_upward,) = gelu_pull(contract_cols(delta_down, w_downward))
-    delta_up = delta_upward.astype(jnp.bfloat16)
-    grad_up = contract_rows(hidden_half, delta_up)
-    delta_hidden = delta_two + contract_cols(delta_up, w_upward)
-    delta_one, delta_gain_one, delta_shift_one = norm_one_pull(delta_hidden)
-    delta_attn = delta_one.astype(jnp.bfloat16)
-    grad_output = contract_rows(context_tok, delta_attn)
-    delta_context = contract_cols(delta_attn, w_output).astype(jnp.bfloat16)
-    delta_joint = back_rows((joint, logsum, delta_context, segment_row, length_row)).reshape(-1, 3 * D)
-    grad_joint = contract_rows(flat_tokens, delta_joint)
-    input_row = (delta_one + contract_cols(delta_joint, w_joint)).astype(jnp.bfloat16)
-    grad_blocks = jnp.concatenate(
-        [
-            into_blocks(grad_joint[:, :D]),
-            into_blocks(grad_joint[:, D : 2 * D]),
-            into_blocks(grad_joint[:, 2 * D :]),
-            into_blocks(grad_output),
-            into_blocks(grad_up),
-            into_blocks(grad_down),
-        ],
-        axis=0,
-    ).astype(jnp.bfloat16)
-    vector_grad = jnp.concatenate([delta_gain_one, delta_shift_one, delta_gain_two, delta_shift_two])
-    slot_index = jnp.arange(48, dtype=jnp.int32)
-    placed = pick_blocks(grad_blocks, slot_index, owner_slot, 1, 0).astype(jnp.bfloat16)
-    extra = jnp.broadcast_to(
-        vector_grad.astype(jnp.bfloat16).reshape(8, 1, 1, BLK), (8, 6, 16, BLK)
-    ).reshape(48, 16, BLK)
-    placed = jnp.concatenate([placed, extra], axis=1)
-    rows_of = lambda row: row.reshape(row_count, token_count, D)
-    total, block_out, input_half = reduce_all(placed, rows_of(block_row), rows_of(input_row))
-    owned = total[:, :BLK].astype(jnp.float32)
-    vector_piece = total[0, BLK].astype(jnp.float32)
-    moment_one, moment_two, left_new, right_new, weights_new = soap_update(
-        owned, slot_weights, first_moment, second_moment, left_stats, right_stats, left_basis, right_basis
-    )
-    vector_one, vector_two, vector_new = adam_update(vector_piece, vector_values, vector_first, vector_second)
-    return (
-        block_out, input_half.astype(jnp.float32), moment_one, moment_two, left_new, right_new, weights_new,
-        weights_new.astype(jnp.bfloat16), vector_one, vector_two, vector_new,
-    )
+    placed, block_row, input_row = run_layer(
+        owner_slot, gathered, token_row.reshape(-1, D), grad_row.reshape(-1, D), segment_ids
+    )
+    total, block_out, input_half = reduce_all(
+        placed, block_row.reshape(tokens.shape), input_row.reshape(tokens.shape)
+    )
+    updated = update_all(
+        total, slot_weights, first_moment, second_moment, left_stats, right_stats, left_basis, right_basis,
+        vector_values, vector_first, vector_second,
+    )
+    vectors = [value.reshape(-1) for value in updated[6:]]
+    return (block_out, input_half.astype(jnp.float32), *updated[:6], *vectors)
 
 
 def solution(mesh):

time: 529 us -> 252 us (0.48); the launches traced: 522 us -> 252 us
  local copies, waits for them, and re-layouts: 164 us -> 5.61 us
  matrix products: 125 us -> 0 us
  Pallas kernels: 167 us -> 242 us
  other arithmetic: 65.3 us -> 3.06 us
    dot_general x24 -> x0, matrix products: 125 us -> none  [the longest x1 18.3 us: fast_device(): upward = jnp.dot(hidden_half, w_upward, preferred_element_type=jnp.float32)]
    pallas_call x1 -> x3, Pallas kernels: 71 us -> 152 us  [the longest x1 70.8 us: gather_all(): pl.pallas_call(gather_kernel, name='gather_all', out_shape=[pltpu.HBM((48...]
    reshape x15 -> x2, local copies, waits for them, and re-layouts: 50.4 us -> 0.01 us  [the longest x1 0.01 us: update_all(): vec_first.reshape(1, BLK)]
    unnamed x167 -> x21, local copies, waits for them, and re-layouts: 43.8 us -> 4.92 us
    gather x2 -> x0, local copies, waits for them, and re-layouts: 25 us -> none  [the longest x1 12.6 us: fast_device(): blocks = jnp.take(gathered, owner_slot, axis=0)[:, :BLK]]
    convert_element_type x7 -> x1, other arithmetic: 24.7 us -> 1.27 us  [fast_device(): return (block_out, input_half.astype(jnp.float32), *updated[:6], *vectors)]
    slice x5 -> x0, local copies, waits for them, and re-layouts: 18.7 us -> none  [the longest x1 8.9 us: split_blocks(): blocks[4 * square + broad:4 * square + 2 * broad]]
    select_n x3 -> x0, other arithmetic: 14.2 us -> none  [the longest x2 14.2 us: fast_device(): blocks = jnp.take(gathered, owner_slot, axis=0)[:, :BLK]]
where the time goes in v2:
time: 252 us
  Pallas kernels  242 us (96%)
  local copies, waits for them, and re-layouts  5.61 us (2%)
  other arithmetic  3.06 us (1%)
    pallas_call x1, Pallas kernels, reduce_all(): pl.pallas_call(reduce_kernel, name='reduce_all', out_shape=[jax.ShapeDtyp...  90.8 us
    pallas_call x1, Pallas kernels, gather_all(): pl.pallas_call(gather_kernel, name='gather_all', out_shape=[pltpu.HBM((48...  70.8 us
    pallas_call x1, Pallas kernels, run_layer(): pl.pallas_call(layer_kernel, name='run_layer', out_shape=[jax.ShapeDtypeS...  66.2 us
    pallas_call x1, Pallas kernels, update_all(): pl.pallas_call(update_kernel, name='update_all', grid=(holding,), out_sha...  14.7 us

profile of v2, /device:TPU:1, one launch (start us, length us, event | category | flops | bytes accessed | tf_op | source)
XLA Modules:
  0.0 251.9 jit_solution(16416387162263806069)
XLA Ops:
  0.6 0.7 reshape.53.vector.vec
  1.3 70.8 %gather_all.1 = (bf16[48,400,384]{2,1,0:T(8,128)(2,1)}, bf16[4,128,768]{2,1,0:T(8,128)(2,1)}, bf16[4,128,768]{2,1,0:T(8,128)(2,1)}) custom-call(f32[6,384,384]{2,1,0:T(8,128)} %weights.3, f32[1,384]{1,0:T(1,128)S(1)} %reshape.53.vector.vec, bf16[4,128,768]{2,1,0:T(8,128)(2,1)} %tokens.1, bf16[4,128,768]{2,1,0:T(8,128)(2,1)} %grads.1), custom_call_target="tpu_custom_call" | custom-call | tf_op jit(solution)/shard_map/gather_all/pallas_call | solution.py:526
  72.1 66.2 %run_layer.1 = (bf16[48,400,384]{2,1,0:T(8,128)(2,1)}, bf16[512,768]{1,0:T(8,128)(2,1)}, bf16[512,768]{1,0:T(8,128)(2,1)}) custom-call(s32[48]{0:T(128)} %owner.1, bf16[48,400,384]{2,1,0:T(8,128)(2,1)} %get-tuple-element.29.weights, bf16[512,768]{1,0:T(8,128)(2,1)} %bitcast.6, bf16[512,768]{1,0:T(8,128)(2,1)} %bitcast.7, s32[4,512]{1,0:T(4,128)} %segments.1), custom_call_target="tpu_custom_call" | custom-call | tf_op jit(solution)/shard_map/run_layer/pallas_call | solution.py:854
  138.3 0.0 copy-start.8
  138.3 0.0 copy-start.9
  138.3 0.0 copy-start
  138.3 0.0 copy-start.1
  138.4 0.0 copy-start.2
  138.4 0.0 copy-start.3
  138.4 90.8 %reduce_all.1 = (bf16[6,400,384]{2,1,0:T(8,128)(2,1)S(1)}, bf16[4,128,768]{2,1,0:T(8,128)(2,1)}, bf16[4,128,768]{2,1,0:T(8,128)(2,1)}) custom-call(bf16[48,400,384]{2,1,0:T(8,128)(2,1)} %get-tuple-element.32.grads, bf16[4,128,768]{2,1,0:T(8,128)(2,1)} %bitcast.4, bf16[4,128,768]{2,1,0:T(8,128)(2,1)} %bitcast.5), custom_call_target="tpu_custom_call" | custom-call | tf_op jit(solution)/shard_map/reduce_all/pallas_call | solution.py:1128
  229.2 0.0 copy-done.8
  229.2 0.0 copy-done.9
  229.2 0.0 copy-done
  229.2 0.0 copy-done.1
  229.2 0.0 copy-done.2
  229.3 0.0 copy-start.4
  229.3 2.0 copy-done.4
  231.3 2.0 copy-done.5
  233.3 14.7 %update_all.1 = (f32[6,384,384]{2,1,0:T(8,128)}, f32[6,384,384]{2,1,0:T(8,128)}, f32[6,384,384]{2,1,0:T(8,128)}, f32[6,384,384]{2,1,0:T(8,128)}, f32[6,384,384]{...) custom-call(bf16[6,400,384]{2,1,0:T(8,128)(2,1)S(1)} %get-tuple-elem, ...), custom_call_target="tpu_custom_call" | custom-call | tf_op jit(solution)/shard_map/update_all/pallas_call | solution.py:1198
  248.0 0.6 reduce
  248.6 0.6 reduce.1
  249.2 0.6 reduce.2
  249.8 1.3 convert_element_type.3
  251.0 0.9 copy.26
  (8 shorter events, 0.0 us)
Async XLA Ops:
  138.3 90.9 %copy-start.8 = (f32[384]{0:T(512)S(1)}, f32[384]{0:T(512)}, u32[]{:S(2)}) copy-start(f32[384]{0:T(512)} %param.27) | copy-start | bytes 4612
  138.3 90.9 %copy-start.9 = (f32[384]{0:T(512)S(1)}, f32[384]{0:T(512)}, u32[]{:S(2)}) copy-start(f32[384]{0:T(512)} %param.28) | copy-start | bytes 4612
  138.3 90.9 %copy-start = (f32[6,384,384]{2,1,0:T(8,128)S(1)}, f32[6,384,384]{2,1,0:T(8,128)}, u32[]{:S(2)}) copy-start(f32[6,384,384]{2,1,0:T(8,128)} %weights.3) | copy-start | bytes 10616836
  138.3 90.9 %copy-start.1 = (f32[6,384,384]{2,1,0:T(8,128)S(1)}, f32[6,384,384]{2,1,0:T(8,128)}, u32[]{:S(2)}) copy-start(f32[6,384,384]{2,1,0:T(8,128)} %first.1) | copy-start | bytes 10616836
  138.4 90.9 %copy-start.2 = (f32[6,384,384]{2,1,0:T(8,128)S(1)}, f32[6,384,384]{2,1,0:T(8,128)}, u32[]{:S(2)}) copy-start(f32[6,384,384]{2,1,0:T(8,128)} %second.1) | copy-start | bytes 10616836
  138.4 90.9 %copy-start.3 = (f32[6,384,384]{2,1,0:T(8,128)S(1)}, f32[6,384,384]{2,1,0:T(8,128)}, u32[]{:S(2)}) copy-start(f32[6,384,384]{2,1,0:T(8,128)} %left.1) | copy-start | bytes 10616836
  229.3 2.0 copy-start.4
  231.3 2.0 copy-start.5
  233.3 16.5 %copy-start.7 = (bf16[4,128,768]{2,1,0:T(8,128)(2,1)S(1)}, bf16[4,128,768]{2,1,0:T(8,128)(2,1)}, u32[]{:S(2)}) copy-start(bf16[4,128,768]{2,1,0:T(8,128)(2,1)} %get-tuple-element.36) | copy-start | bytes 2359300
  233.3 17.8 %copy-start.6 = (bf16[4,128,768]{2,1,0:T(8,128)(2,1)S(1)}, bf16[4,128,768]{2,1,0:T(8,128)(2,1)}, u32[]{:S(2)}) copy-start(bf16[4,128,768]{2,1,0:T(8,128)(2,1)} %get-tuple-element.58) | copy-start | bytes 2359300

commit v3 on v2

--- a/solution.py
+++ b/solution.py
@@ -556,17 +556,15 @@
 EPS = 1e-06
 
 
-def erf_of(x):
-    x = jnp.clip(x, -3.832506856900711, 3.832506856900711)
-    s = x * x
-    top = 0.00022905065861350646
-    for term in (0.0034082910107109506, 0.050955695062380861, 0.18520832239976145, 1.128379143519084):
-        top = top * s + term
-    bottom = -1.1791602954361697e-7
-    for term in (0.000023547966471313185, 0.0010179625278914885, 0.014070470171167667,
-                 0.11098505178285362, 0.49746925110067538, 1.0):
-        bottom = bottom * s + term
-    return x * top / bottom
+def gelu_of(u):
+    bell = jnp.exp(-0.5 * u * u)
+    t = 1.0 / (1.0 + (0.3275911 / math.sqrt(2.0)) * jnp.abs(u))
+    tail = 0.5 * 1.061405429
+    for term in (-1.453152027, 1.421413741, -0.284496736, 0.254829592):
+        tail = tail * t + 0.5 * term
+    tail = tail * t * bell
+    below = jnp.where(u >= 0.0, 1.0 - tail, tail)
+    return (u * below).astype(jnp.bfloat16), below + u * (bell * (1.0 / math.sqrt(2.0 * math.pi)))
 
 
 def dot_nn(a, b):
@@ -583,8 +581,8 @@
 
 def layer_kernel(
     owner, weights, tokens, dy_ref, segments, grads, block_out, input_half,
-    wqkv, wo, w1, w2, gains, qkv, probs, context, hidden, hidden16, norm1, act, slope, acc, dz, dz16,
-    dqkv, dup, stage, vecs, spread, w_sem, g_sem, v_sem,
+    wqkv, wo, w1, w2, gains, qkv, probs, shares, held, context, hidden, hidden16, norm1, act, slope, acc, dz, dz16,
+    dqkv, dup, stage, flipped, flipped_hidden, ups, vecs, spread, w_sem, g_sem, v_sem,
 ):
     half = jnp.bfloat16
     sp = lax.axis_index("sp")
@@ -626,6 +624,7 @@
     for item in copies[:12]:
         item.wait()
     x = tokens[...]
+    flipped[...] = jnp.transpose(x)
     for part in range(3):
         block = dot_nn(x, wqkv[part])
         if part == 0:
@@ -653,12 +652,12 @@
             for h in range(2):
                 scores = dot_nt(jnp.where(lows[h], qs, jnp.zeros_like(qs)), ks)
                 scores = jnp.where(mask, scores, -1e30)
-                top = jnp.max(scores, axis=1, keepdims=True)
-                raised = jnp.exp(scores - top)
-                prob = raised * (1.0 / jnp.sum(raised, axis=1, keepdims=True))
-                probs[p, 2 * part + h] = prob
-                outs.append(dot_nn(prob.astype(half), vs))
-            context[p, pl.ds(part * 256, 256)] = jnp.where(lows[0], outs[0], outs[1]).astype(half)
+                raised = jnp.exp(scores - jnp.max(scores, axis=1, keepdims=True)).astype(half)
+                probs[p, 2 * part + h] = raised
+                outs.append(dot_nn(raised, jnp.where(lows[h], vs, jnp.ones_like(vs))))
+            inverse = 1.0 / pltpu.roll(jnp.where(lows[0], outs[1], outs[0]), 64, 1)
+            shares[p, pl.ds(part * 256, 256)] = inverse
+            context[p, pl.ds(part * 256, 256)] = (jnp.where(lows[0], outs[0], outs[1]) * inverse).astype(half)
         return carry
 
     lax.fori_loop(0, 6, attend, 0)
@@ -692,17 +691,15 @@
     for item in copies[16:]:
         item.wait()
 
-    def forward(j, carry):
-        up = dot_nn(hidden16[...], w1[j])
-        phi_big = 0.5 + 0.5 * erf_of(up * (1.0 / math.sqrt(2.0)))
-        value = (up * phi_big).astype(half)
-        slope[j] = phi_big + up * (jnp.exp(-0.5 * up * up) * (1.0 / math.sqrt(2.0 * math.pi)))
-        act[j] = value
-        part = dot_nn(value, w2[j])
-        hidden[...] += part
-        return carry
-
-    lax.fori_loop(0, 4, forward, 0)
+    flipped_hidden[...] = jnp.transpose(hidden16[...])
+    ups[0] = dot_nn(hidden16[...], w1[0])
+    for j in range(5):
+        if j < 3:
+            ups[(j + 1) % 2] = dot_nn(hidden16[...], w1[j + 1])
+        if j < 4:
+            act[j], slope[j] = gelu_of(ups[j % 2])
+        if j > 0:
+            hidden[...] += dot_nn(act[j - 1], w2[j - 1])
 
     vecs[...] = jnp.zeros_like(vecs)
 
@@ -757,7 +754,7 @@
 
         stage[2 * (j % 2)] = dot_tn(act[j], ddown).astype(half)
         flush(2 * (j % 2), lambda r, q: 32 + (2 * j + r) * 2 + q)
-        stage[2 * (j % 2) + 1] = dot_tn(hidden16[...], delta).astype(half)
+        stage[2 * (j % 2) + 1] = dot_nn(flipped_hidden[...], delta).astype(half)
         flush(2 * (j % 2) + 1, lambda r, q: 16 + r * 8 + 2 * j + q)
         dz[...] += dot_nt(delta, w1[j])
         return carry
@@ -784,6 +781,7 @@
     flush(0, lambda r, q: 12 + r * 2 + q)
     dcontext = dot_nt(dattn, wo[...]).astype(half)
     for p in range(6):
+        held[p] = context[p]
         context[p] = dcontext[:, p * PAIR : (p + 1) * PAIR]
 
     def attend_back(p, carry):
@@ -796,12 +794,15 @@
             ks = k2[part * PAIR : part * PAIR + SPAN]
             vs = v2[part * PAIR : part * PAIR + SPAN]
             dvs, dqs, dks = [], [], []
+            share = shares[p, pl.ds(part * 256, 256)]
+            scaled = (ds.astype(jnp.float32) * share).astype(half)
+            weight = scaled.astype(jnp.float32) * held[p, pl.ds(part * 256, 256)].astype(jnp.float32)
             for h in range(2):
-                prob = probs[p, 2 * part + h]
-                dprob = dot_nt(jnp.where(lows[h], ds, jnp.zeros_like(ds)), vs)
-                product = prob * dprob
-                dscore = (product - prob * jnp.sum(product, axis=1, keepdims=True)).astype(half)
-                dvs.append(dot_tn(prob.astype(half), ds))
+                raised = probs[p, 2 * part + h]
+                dprob = dot_nt(jnp.where(lows[h], scaled, jnp.zeros_like(scaled)), vs)
+                centre = jnp.sum(jnp.where(lows[h], weight, 0.0), axis=1, keepdims=True)
+                dscore = (raised.astype(jnp.float32) * (dprob - centre)).astype(half)
+                dvs.append(dot_tn(raised, scaled))
                 dqs.append(dot_nn(dscore, ks))
                 dks.append(dot_tn(dscore, qs))
             dqkv[p, pl.ds(part * 256, 256)] = (
@@ -817,7 +818,7 @@
 
     for part in range(3):
         delta = jnp.concatenate([dqkv[part * 6 + p] for p in range(6)], axis=1)
-        stage[1 + part] = dot_tn(x, delta).astype(half)
+        stage[1 + part] = dot_nn(flipped[...], delta).astype(half)
         flush(1 + part, lambda r, q: part * 4 + r * 2 + q)
         dz[...] += dot_nt(delta, wqkv[part])
 
@@ -868,7 +869,9 @@
             pltpu.VMEM((4, D, D), half),
             pltpu.VMEM((4, 16, D), half),
             pltpu.VMEM((18, ROW, PAIR), half),
-            pltpu.VMEM((6, 4, 256, SPAN), full),
+            pltpu.VMEM((6, 4, 256, SPAN), half),
+            pltpu.VMEM((6, ROW, PAIR), full),
+            pltpu.VMEM((6, ROW, PAIR), half),
             pltpu.VMEM((6, ROW, PAIR), half),
             pltpu.VMEM((ROW, D), full),
             pltpu.VMEM((ROW, D), half),
@@ -881,6 +884,9 @@
             pltpu.VMEM((18, ROW, PAIR), half),
             pltpu.VMEM((2, ROW, PAIR), full),
             pltpu.VMEM((4, D, D), half),
+            pltpu.VMEM((D, ROW), half),
+            pltpu.VMEM((D, ROW), half),
+            pltpu.VMEM((2, ROW, D), full),
             pltpu.VMEM((4, 8, D), full),
             pltpu.VMEM((ROW, PAIR), full),
             dma((48,)),
@@ -893,23 +899,42 @@
 
 BLANK = BLK + 16
 HALF = BLK // 2
-
-
-def reduce_kernel(
-    grads, rows_a, rows_b, total, land_a, land_b,
-    mine0, mine1, mine2, mine3, core0, core1, core2, core3, cross, side0, side1, side2,
-    line0, line1, line2, last0, last1,
-    load_sem, core_send, core_recv, x_send, x_recv, y_send, y_recv, z_send, z_recv,
-    last_send, last_recv, give_send, give_recv, keep_sem, row_send, row_recv, row_keep,
-):
+STREAMS = {
+    "A0": (BLANK, 0, True, True),
+    "A1": (HALF, 0, True, True),
+    "A2": (HALF, HALF, True, False),
+    "O": (HALF, 0, False, True),
+    "XO": (HALF, 0, False, True),
+}
+TASKS = (
+    ("Y", "A1", 1), ("Y", "A1", 0), ("Z", "A2", 0, 0), ("Y", "A0", 0), ("X", "O", 0, 1), ("X", "O", 0, 0),
+    ("Z", "A2", 1, 1), ("X", "O", 1, 1), ("Y", "A0", 2), ("X", "O", 1, 0), ("R", 1), ("Z", "A2", 0, 1),
+    ("Z", "A2", 2, 1), ("Z", "A2", 3, 0), ("X", "O", 2, 1), ("R", 0), ("Z", "A2", 1, 0), ("Z", "A2", 2, 0),
+    ("Z", "A2", 3, 1), ("Y", "A0", 1), ("X", "O", 3, 1), ("X", "O", 2, 0), ("Y", "O", 0), ("C", "A0", 0),
+    ("Y", "O", 1), ("X", "O", 3, 0), ("C", "A1", 0), ("F1", "A2"), ("Y", "A1", 2), ("Y", "A0", 3), ("C", "A0", 1),
+    ("C", "A0", 2), ("Y", "A1", 3), ("C", "O", 0), ("Y", "O", 2), ("F", "A2"), ("Y", "O", 3), ("C", "A1", 1),
+    ("C", "A0", 3), ("F", "A0"), ("C", "O", 1), ("C", "O", 2), ("C", "A1", 2), ("C", "O", 3), ("C", "A1", 3),
+    ("F", "O"), ("L", "A2"), ("L", "A0"), ("F", "A1"), ("L", "O"), ("L", "A1"),
+)
+
+
+def reduce_kernel(grads, rows_a, rows_b, total, land_a, land_b, *scratch):
     z, y, x, c = place()
     dp = z * 2 + y
     sp = x * 2 + c
-    mine = (mine0, mine1, mine2, mine3)
-    core = (core0, core1, core2, core3)
-    side = (side0, side1, side2)
-    line = (line0, line1, line2)
-    last = (last0, last1)
+    names = list(STREAMS)
+    moving = [name for name in names if name != "XO"]
+    planes = [name for name in moving if STREAMS[name][2]]
+    scratch = list(scratch)
+
+    def take(keys):
+        return {key: scratch.pop(0) for key in keys}
+
+    mine, core, side, line, last = take(names), take(names), take(moving), take(moving), take(planes)
+    cross, = take(["cross"]).values()
+    load_sem, core_send, core_recv = take(names), take(names), take(names)
+    y_send, y_recv, z_send, z_recv = take(moving), take(moving), take(moving), take(moving)
+    x_send, x_recv, last_send, last_recv, give_send, give_recv, keep_sem, row_send, row_recv, row_keep = scratch
     high = z // 2
     order = (3 - 3 * high, 2 - high, 1 - z + 4 * high, z)
     twin = (dp, (1 - x) * 2 + c)
@@ -917,13 +942,13 @@
     beside = (z * 2 + 1 - y, sp)
     inner = (z > 0) & (z < NZ - 1)
 
-    def view(ref, stream, dest, core_of):
+    def view(ref, name, dest, core_of):
         base = dest * 6
-        if stream == 0:
+        if name == "A0":
             return ref.at[base + core_of, pl.ds(0, BLANK)]
-        if stream == 1:
-            return ref.at[base + 2 + core_of, pl.ds(0, BLK)]
-        slot = base + (4 + x if stream == 2 else 5 - x)
+        if name in ("A1", "A2"):
+            return ref.at[base + 2 + core_of, pl.ds(STREAMS[name][1], HALF)]
+        slot = base + (4 + x if name == "O" else 5 - x)
         return ref.at[slot, pl.ds(pl.multiple_of(core_of * HALF, HALF), HALF)]
 
     def remote(src, dst, send, recv, target):
@@ -932,25 +957,23 @@
             device_id=target, device_id_type=MESH,
         )
 
-    def load(stream, dest):
-        return pltpu.make_async_copy(
-            view(grads, stream, dest, c), mine[stream].at[dest], load_sem.at[stream, dest]
+    def load(name, dest):
+        return pltpu.make_async_copy(view(grads, name, dest, c), mine[name].at[dest], load_sem[name].at[dest])
+
+    def to_mate(name, dest):
+        return remote(
+            view(grads, name, dest, 1 - c), core[name].at[dest],
+            core_send[name].at[dest], core_recv[name].at[dest], mate,
         )
 
-    def to_mate(stream, dest):
+    def to_twin(dest):
+        return remote(mine["XO"].at[dest], cross.at[dest], x_send.at[dest], x_recv.at[dest], twin)
+
+    def to_side(name, goal):
+        at = goal if STREAMS[name][3] else 0
         return remote(
-            view(grads, stream, dest, 1 - c), core[stream].at[dest],
-            core_send.at[stream, dest], core_recv.at[stream, dest], mate,
-        )
-
-    def to_twin(dest):
-        return remote(mine3.at[dest], cross.at[dest], x_send.at[dest], x_recv.at[dest], twin)
-
-    def to_side(stream, goal):
-        dest = goal * 2 + 1 - y
-        return remote(
-            mine[stream].at[dest], side[stream].at[goal],
-            y_send.at[stream, goal], y_recv.at[stream, goal], beside,
+            mine[name].at[goal * 2 + 1 - y], side[name].at[at],
+            y_send[name].at[at], y_recv[name].at[at], beside,
         )
 
     def row_copy(which, source, landing, step, arrival):
@@ -961,21 +984,19 @@
             row_send.at[which, step - 1], row_recv.at[which, at], (dp, peer),
         )
 
-    sequence = []
-    for i in range(4):
-        away = order[i] * 2 + 1 - y
-        sequence += [(3, away), (0, away), (1, away)]
-    for i in range(4):
-        sequence += [(3, order[i] * 2 + y)]
-    for i in range(4):
-        sequence += [(2, order[i] * 2 + 1 - y)]
-    for i in range(4):
-        home = order[i] * 2 + y
-        sequence += [(0, home), (1, home)]
-    for i in range(4):
-        sequence += [(2, order[i] * 2 + y)]
-    for stream, dest in sequence:
-        load(stream, dest).start()
+    def column_of(flag):
+        return y if flag == 0 else 1 - y
+
+    def dest_of(task):
+        if task[0] in ("X", "Z"):
+            return order[task[2]] * 2 + column_of(task[3])
+        return order[task[2]] * 2 + (1 - y if task[0] == "Y" else y)
+
+    sequence = [
+        ("XO" if task[0] == "X" else task[1], dest_of(task)) for task in TASKS if task[0] in ("X", "Y", "C", "Z")
+    ]
+    for name, dest in sequence:
+        load(name, dest).start()
     keeps = [
         pltpu.make_async_copy(rows_a.at[sp], land_a.at[sp], row_keep.at[0]),
         pltpu.make_async_copy(rows_b.at[sp], land_b.at[sp], row_keep.at[1]),
@@ -983,137 +1004,144 @@
     for keep in keeps:
         keep.start()
     greet(z, y, x, c)
-    for stream, dest in sequence:
-        to_mate(stream, dest).start()
-
-    def merge(stream, dest):
-        load(stream, dest).wait()
-        to_mate(stream, dest).wait_recv()
-        mine[stream][dest] = mine[stream][dest] + core[stream][dest]
-
-    def along(stream, goal):
-        dest = goal * 2 + y
+    for name, dest in sequence:
+        to_mate(name, dest).start()
+
+    def merge(name, dest):
+        load(name, dest).wait()
+        to_mate(name, dest).wait_recv()
+        value = mine[name][dest] + core[name][dest]
+        if name == "O":
+            to_twin(dest).wait_recv()
+            value = value + cross[dest]
+        mine[name][dest] = value
+
+    def hop(name, goal, column, way, target):
+        lane = goal if STREAMS[name][3] else goal * 2 + column
+        return remote(
+            mine[name].at[goal * 2 + column], line[name].at[way, lane],
+            z_send[name].at[lane], z_recv[name].at[way, lane], target,
+        )
+
+    def along(name, goal, column):
+        dest = goal * 2 + column
         upward = (goal > z).astype(jnp.int32)
         step = 2 * upward - 1
         way = 1 - upward
-        item = remote(
-            mine[stream].at[dest], line[stream].at[way, goal],
-            z_send.at[stream, goal], z_recv.at[stream, way, goal], (dp + 2 * step, sp),
-        )
+        item = hop(name, goal, column, way, (dp + 2 * step, sp))
+        lane = goal if STREAMS[name][3] else dest
 
         @pl.when(inner)
         def _():
             item.wait_recv()
-            mine[stream][dest] = mine[stream][dest] + line[stream][way, goal]
+            mine[name][dest] = mine[name][dest] + line[name][way, lane]
 
         item.start()
 
-    def settle(stream):
+    def settle(name, column):
+        dest = z * 2 + column
+        lane = z if STREAMS[name][3] else dest
         for way, valid, step in ((0, z > 0, 1), (1, z < NZ - 1, -1)):
             @pl.when(valid)
             def _():
-                remote(
-                    mine[stream].at[dp], line[stream].at[way, z],
-                    z_send.at[stream, z], z_recv.at[stream, way, z], (dp - 2 * step, sp),
-                ).wait_recv()
-                mine[stream][dp] = mine[stream][dp] + line[stream][way, z]
-
-    for i in range(4):
-        away = order[i] * 2 + 1 - y
-        merge(3, away)
-        to_twin(away).start()
-        for stream in (0, 1):
-            merge(stream, away)
-            to_side(stream, order[i]).start()
-    for i in range(4):
-        home = order[i] * 2 + y
-        merge(3, home)
-        to_twin(home).start()
-    for step in (2, 3, 1):
-        row_copy(0, rows_a, land_a, step, False).start()
-    for i in range(4):
-        away = order[i] * 2 + 1 - y
-        merge(2, away)
-        to_twin(away).wait_recv()
-        mine2[away] = mine2[away] + cross[away]
-        to_side(2, order[i]).start()
-        home = order[i] * 2 + y
-        for stream in (0, 1):
-            merge(stream, home)
-            to_side(stream, order[i]).wait_recv()
-            mine[stream][home] = mine[stream][home] + side[stream][order[i]]
-            if i < 3:
-                along(stream, order[i])
-    for step in (2, 3, 1):
-        row_copy(1, rows_b, land_b, step, False).start()
-    for i in range(4):
-        home = order[i] * 2 + y
-        merge(2, home)
-        to_twin(home).wait_recv()
-        mine2[home] = mine2[home] + cross[home]
-        to_side(2, order[i]).wait_recv()
-        mine2[home] = mine2[home] + side2[order[i]]
-        if i < 3:
-            along(2, order[i])
-
-    def swap_last(stream):
-        return remote(
-            mine[stream].at[dp], last[stream], last_send.at[stream], last_recv.at[stream], twin
-        )
-
-    for stream in (0, 1):
-        settle(stream)
-        swap_last(stream).start()
-    settle(2)
-
-    def place_of(stream, core_of):
-        return view(total, stream, 0, core_of)
-
-    def give(stream, index, target, source, core_of):
-        return remote(
-            source, place_of(stream, core_of), give_send.at[index], give_recv.at[index], target
-        )
-
-    own_twin = give(2, 0, twin, mine2.at[dp], c)
-    own_twin.start()
-    own_mate = give(2, 1, mate, mine2.at[dp], c)
-    own_mate.start()
-    kept = [pltpu.make_async_copy(mine2.at[dp], place_of(2, c), keep_sem.at[2])]
-    kept[0].start()
-    gifts = [own_twin, own_mate]
-    for stream in (0, 1):
-        swap_last(stream).wait_recv()
-        core[stream][dp] = mine[stream][dp] + last[stream][...]
-        gift = give(stream, 2 + stream, mate, core[stream].at[dp], c)
-        gift.start()
-        gifts.append(gift)
-        keep = pltpu.make_async_copy(core[stream].at[dp], place_of(stream, c), keep_sem.at[stream])
-        keep.start()
-        kept.append(keep)
-    give(3, 0, twin, place_of(3, c), c).wait_recv()
-    passed = give(3, 4, mate, place_of(3, c), c)
-    passed.start()
-    gifts.append(passed)
-    for stream, index in ((2, 1), (0, 2), (1, 3), (3, 4)):
-        give(stream, index, mate, place_of(stream, 1 - c), 1 - c).wait_recv()
+                hop(name, z, column, way, (dp - 2 * step, sp)).wait_recv()
+                mine[name][dest] = mine[name][dest] + line[name][way, lane]
+
+    def swap_last(name):
+        at = planes.index(name)
+        return remote(mine[name].at[dp], last[name], last_send.at[at], last_recv.at[at], twin)
+
+    def place_of(name, core_of):
+        return view(total, name, 0, core_of)
+
+    gift_at = {name: at for at, name in enumerate(planes + ["O", "twin", "XO"])}
+
+    def give(name, key, target, source, core_of):
+        at = gift_at[key]
+        return remote(source, place_of(name, core_of), give_send.at[at], give_recv.at[at], target)
+
+    gifts, kept = [], []
+
+    def hand_on(name, key, target, source):
+        item = give(name, key, target, source, c)
+        item.start()
+        gifts.append(item)
+
+    def keep_here(name, source):
+        item = pltpu.make_async_copy(source, place_of(name, c), keep_sem.at[gift_at[name]])
+        item.start()
+        kept.append(item)
+
+    for task in TASKS:
+        kind, name = task[0], task[1]
+        if kind == "R":
+            source, landing = ((rows_a, land_a), (rows_b, land_b))[name]
+            for step in (2, 3, 1):
+                row_copy(name, source, landing, step, False).start()
+        elif kind == "X":
+            merge("XO", dest_of(task))
+            to_twin(dest_of(task)).start()
+        elif kind == "Y":
+            merge(name, dest_of(task))
+            to_side(name, order[task[2]]).start()
+        elif kind == "C":
+            dest = dest_of(task)
+            merge(name, dest)
+            to_side(name, order[task[2]]).wait_recv()
+            mine[name][dest] = mine[name][dest] + side[name][order[task[2]]]
+            if task[2] < 3:
+                along(name, order[task[2]], y)
+        elif kind == "Z":
+            merge(name, dest_of(task))
+            if task[2] < 3:
+                along(name, order[task[2]], column_of(task[3]))
+        elif kind == "F1":
+            settle(name, 1 - y)
+            to_side(name, z).start()
+        elif kind == "F":
+            settle(name, y)
+            if not STREAMS[name][3]:
+                to_side(name, z).wait_recv()
+                mine[name][dp] = mine[name][dp] + side[name][0]
+            if name in planes:
+                swap_last(name).start()
+            else:
+                hand_on(name, "twin", twin, mine[name].at[dp])
+                hand_on(name, "O", mate, mine[name].at[dp])
+                keep_here(name, mine[name].at[dp])
+        elif kind == "L":
+            if name in planes:
+                swap_last(name).wait_recv()
+                core[name][dp] = mine[name][dp] + last[name][...]
+                hand_on(name, name, mate, core[name].at[dp])
+                keep_here(name, core[name].at[dp])
+            else:
+                give("XO", "twin", twin, place_of("XO", c), c).wait_recv()
+                hand_on("XO", "XO", mate, place_of("XO", c))
+
+    for name in planes + ["O", "XO"]:
+        give(name, name, mate, place_of(name, 1 - c), 1 - c).wait_recv()
     for step in (2, 3, 1):
         for which, source, landing in ((0, rows_a, land_a), (1, rows_b, land_b)):
             row_copy(which, source, landing, step, True).wait_recv()
             row_copy(which, source, landing, step, False).wait_send()
-    for stream, dest in sequence:
-        to_mate(stream, dest).wait_send()
+    for name, dest in sequence:
+        to_mate(name, dest).wait_send()
     for i in range(4):
-        for side_of in (0, 1):
-            to_twin(order[i] * 2 + side_of).wait_send()
-        for stream in range(3):
-            to_side(stream, order[i]).wait_send()
-            if i < 3:
-                remote(
-                    mine[stream].at[order[i] * 2 + y], line[stream].at[0, order[i]],
-                    z_send.at[stream, order[i]], z_recv.at[stream, 0, order[i]], twin,
-                ).wait_send()
-    for stream in (0, 1):
-        swap_last(stream).wait_send()
+        for column in (0, 1):
+            to_twin(order[i] * 2 + column).wait_send()
+        for name in moving:
+            if STREAMS[name][3]:
+                to_side(name, order[i]).wait_send()
+                if i < 3:
+                    hop(name, order[i], y, 0, twin).wait_send()
+            elif i < 3:
+                for column in (0, 1):
+                    hop(name, order[i], column, 0, twin).wait_send()
+            else:
+                to_side(name, z).wait_send()
+    for name in planes:
+        swap_last(name).wait_send()
     for item in gifts:
         item.wait_send()
     for item in kept + keeps:
@@ -1121,10 +1149,16 @@
 
 
 def reduce_all(grads, rows_a, rows_b):
-    anywhere = pl.BlockSpec(memory_space=pltpu.HBM)
+    anywhere = pl.BlockSpec(memory_space=pl.ANY)
     half = jnp.bfloat16
-    heights = (BLANK, BLK, HALF, HALF)
     dma = pltpu.SemaphoreType.DMA
+    moving = [name for name in STREAMS if name != "XO"]
+    planes = [name for name in moving if STREAMS[name][2]]
+
+    def buffers(shapes):
+        return [pltpu.VMEM((*lead, STREAMS[name][0], BLK), half) for name, lead in shapes]
+
+    first = {name: STREAMS[name][3] for name in moving}
     return pl.pallas_call(
         reduce_kernel,
         name="reduce_all",
@@ -1135,79 +1169,126 @@
         ],
         in_specs=[anywhere] * 3,
         out_specs=[anywhere] * 3,
-        scratch_shapes=[pltpu.VMEM((8, h, BLK), half) for h in heights]
-        + [pltpu.VMEM((8, h, BLK), half) for h in heights]
-        + [pltpu.VMEM((8, HALF, BLK), half)]
-        + [pltpu.VMEM((4, h, BLK), half) for h in heights[:3]]
-        + [pltpu.VMEM((2, 4, h, BLK), half) for h in heights[:3]]
-        + [pltpu.VMEM((h, BLK), half) for h in heights[:2]]
+        scratch_shapes=buffers([(name, (8,)) for name in STREAMS] * 2)
+        + buffers([(name, (4 if first[name] else 1,)) for name in moving])
+        + buffers([(name, (2, 4 if first[name] else 8)) for name in moving])
+        + buffers([(name, ()) for name in planes])
+        + buffers([("O", (8,))])
+        + [dma((8,))] * (3 * len(STREAMS))
+        + [dma((4 if first[name] else 1,)) for name in moving] * 2
+        + [dma((4 if first[name] else 8,)) for name in moving]
+        + [dma((2, 4 if first[name] else 8)) for name in moving]
         + [
-            dma((4, 8)), dma((4, 8)), dma((4, 8)), dma((8,)), dma((8,)), dma((3, 4)), dma((3, 4)),
-            dma((3, 4)), dma((3, 2, 4)), dma((2,)), dma((2,)), dma((5,)), dma((5,)), dma((3,)),
-            dma((2, 3)), dma((2, 4)), dma((2,)),
+            dma((8,)), dma((8,)), dma((len(planes),)), dma((len(planes),)), dma((len(planes) + 3,)),
+            dma((len(planes) + 3,)), dma((len(planes) + 1,)), dma((2, 3)), dma((2, 4)), dma((2,)),
         ],
         compiler_params=pltpu.CompilerParams(
-            collective_id=1, has_side_effects=True, vmem_limit_bytes=30 << 20
+            collective_id=1, has_side_effects=True, vmem_limit_bytes=28 << 20
         ),
     )(in_hbm(grads), in_hbm(rows_a), in_hbm(rows_b))
 
 
 CORRECT = 1.0 - 0.5**STEP
+GROUP = 2
 
 
 def update_kernel(
-    total, weights, first, second, left, right, left_rot, right_rot, vec_grad, vec, vec_first, vec_second,
+    total, weights, first, second, left, right, left_rot, right_rot, vec, vec_first, vec_second, land_a, land_b,
     moment_one, moment_two, left_new, right_new, weights_new, weights_half, vector_one, vector_two, vector_new,
+    rows_a, rows_b, held, narrow, wide, stage, stage_half, out_sem, sems,
 ):
     half = jnp.bfloat16
-    grad = total[0, :BLK, :]
-    left_new[0] = 0.95 * left[0] + 0.05 * dot_nt(grad, grad)
-    right_new[0] = 0.95 * right[0] + 0.05 * dot_tn(grad, grad)
-    rot_l = left_rot[0].astype(half)
-    rot_r = right_rot[0].astype(half)
-    turned = dot_nn(dot_tn(rot_l, grad).astype(half), rot_r)
-    one = 0.5 * first[0] + 0.5 * turned
-    two = 0.5 * second[0] + 0.5 * turned * turned
-    moment_one[0] = one
-    moment_two[0] = two
-    ratio = (one / CORRECT) / (jnp.sqrt(two / CORRECT) + 1e-08)
-    stepped = dot_nt(dot_nn(rot_l, ratio.astype(half)).astype(half), rot_r)
-    fresh = weights[0] - rate_matrix * stepped
-    weights_new[0] = fresh
-    weights_half[0] = fresh.astype(half)
-
-    @pl.when(pl.program_id(0) == 0)
-    def _():
-        slope = vec_grad[0, :1, :].astype(jnp.float32)
-        vec_one = 0.5 * vec_first[...] + 0.5 * slope
-        vec_two = 0.5 * vec_second[...] + 0.5 * slope * slope
-        vector_one[...] = vec_one
-        vector_two[...] = vec_two
-        vector_new[...] = vec[...] - rate_vector * (
-            (vec_one / CORRECT) / (jnp.sqrt(vec_two / CORRECT) + 1e-08)
-        )
-
-
-def update_all(total, weights, first, second, left, right, left_rot, right_rot, vec, vec_first, vec_second):
+    take_a = pltpu.make_async_copy(land_a, held, sems.at[0])
+    give_a = pltpu.make_async_copy(held, rows_a, sems.at[3])
+    take_b = pltpu.make_async_copy(land_b, narrow, sems.at[1])
+    give_b = pltpu.make_async_copy(wide, rows_b, sems.at[2])
+    take_b.start()
+    take_a.start()
+    slope = total[0, pl.ds(BLK, 1), :].astype(jnp.float32)
+    vec_one = 0.5 * vec_first[...] + 0.5 * slope
+    vec_two = 0.5 * vec_second[...] + 0.5 * slope * slope
+    vector_one[...] = vec_one
+    vector_two[...] = vec_two
+    vector_new[...] = vec[...] - rate_vector * (
+        (vec_one / CORRECT) / (jnp.sqrt(vec_two / CORRECT) + 1e-08)
+    )
+    targets = (left_new, right_new, moment_one, moment_two, weights_new)
+
+    def outputs(i):
+        copies = [
+            pltpu.make_async_copy(stage.at[k, i], target.at[i], out_sem.at[i, k])
+            for k, target in enumerate(targets)
+        ]
+        return copies + [pltpu.make_async_copy(stage_half.at[i], weights_half.at[i], out_sem.at[i, 5])]
+
+    def blocks(pair, carry):
+        for i in [pair * GROUP + k for k in range(GROUP)]:
+            grad = total[i, :BLK, :]
+            rot_l = left_rot[i].astype(half)
+            rot_r = right_rot[i].astype(half)
+            turned = dot_nn(dot_tn(rot_l, grad).astype(half), rot_r)
+            stage[0, i] = 0.95 * left[i] + 0.05 * dot_nt(grad, grad)
+            one = 0.5 * first[i] + 0.5 * turned
+            two = 0.5 * second[i] + 0.5 * turned * turned
+            stage[2, i] = one
+            stage[3, i] = two
+            ratio = (one / CORRECT) / (jnp.sqrt(two / CORRECT) + 1e-08)
+            stage[1, i] = 0.95 * right[i] + 0.05 * dot_tn(grad, grad)
+            stepped = dot_nt(dot_nn(rot_l, ratio.astype(half)).astype(half), rot_r)
+            fresh = weights[i] - rate_matrix * stepped
+            stage[4, i] = fresh
+            stage_half[i] = fresh.astype(half)
+        for i in [pair * GROUP + k for k in range(GROUP)]:
+            for item in outputs(i):
+                item.start()
+
+        @pl.when(pair == 0)
+        def _():
+            take_a.wait()
+            give_a.start()
+            take_b.wait()
+            for r in range(narrow.shape[0]):
+                wide[r] = narrow[r].astype(jnp.float32)
+            give_b.start()
+
+        return carry
+
+    lax.fori_loop(0, weights.shape[0] // GROUP, blocks, 0)
+    for i in range(weights.shape[0]):
+        for item in outputs(i):
+            item.wait()
+    give_a.wait()
+    give_b.wait()
+
+
+def update_all(
+    total, weights, first, second, left, right, left_rot, right_rot, vec, vec_first, vec_second, land_a, land_b
+):
     full = jnp.float32
-    holding = weights.shape[0]
-    block = pl.BlockSpec((1, BLK, BLK), lambda i: (i, 0, 0))
-    row = pl.BlockSpec((1, BLK), lambda i: (0, 0))
+    vmem = pl.BlockSpec(memory_space=pltpu.VMEM)
+    anywhere = pl.BlockSpec(memory_space=pl.ANY)
     vector = jax.ShapeDtypeStruct((1, BLK), full)
-    matrix = jax.ShapeDtypeStruct(weights.shape, full)
+    matrix = pltpu.HBM(weights.shape, full)
     return pl.pallas_call(
         update_kernel,
         name="update_all",
-        grid=(holding,),
-        out_shape=[matrix] * 5 + [jax.ShapeDtypeStruct(weights.shape, jnp.bfloat16)] + [vector] * 3,
-        in_specs=[pl.BlockSpec((1, PITCH, BLK), lambda i: (i, 0, 0))]
-        + [block] * 7
-        + [pl.BlockSpec((1, 16, BLK), lambda i: (0, BLK // 16, 0)), row, row, row],
-        out_specs=[block] * 6 + [row] * 3,
+        out_shape=[matrix] * 5 + [pltpu.HBM(weights.shape, jnp.bfloat16)] + [vector] * 3
+        + [pltpu.HBM(land_a.shape, jnp.bfloat16), pltpu.HBM(land_b.shape, full)],
+        in_specs=[vmem] * 11 + [anywhere] * 2,
+        out_specs=[anywhere] * 6 + [vmem] * 3 + [anywhere] * 2,
+        scratch_shapes=[
+            pltpu.VMEM(land_a.shape, jnp.bfloat16),
+            pltpu.VMEM(land_b.shape, jnp.bfloat16),
+            pltpu.VMEM(land_b.shape, full),
+            pltpu.VMEM((5, *weights.shape), full),
+            pltpu.VMEM(weights.shape, jnp.bfloat16),
+            pltpu.SemaphoreType.DMA((weights.shape[0], 6)),
+            pltpu.SemaphoreType.DMA((4,)),
+        ],
         compiler_params=pltpu.CompilerParams(vmem_limit_bytes=30 << 20),
     )(
-        total, weights, first, second, left, right, left_rot, right_rot, total,
-        vec.reshape(1, BLK), vec_first.reshape(1, BLK), vec_second.reshape(1, BLK),
+        total, weights, first, second, left, right, left_rot, right_rot,
+        vec.reshape(1, BLK), vec_first.reshape(1, BLK), vec_second.reshape(1, BLK), in_hbm(land_a), in_hbm(land_b),
     )
 
 
@@ -1219,15 +1300,15 @@
     placed, block_row, input_row = run_layer(
         owner_slot, gathered, token_row.reshape(-1, D), grad_row.reshape(-1, D), segment_ids
     )
-    total, block_out, input_half = reduce_all(
+    total, block_land, input_land = reduce_all(
         placed, block_row.reshape(tokens.shape), input_row.reshape(tokens.shape)
     )
     updated = update_all(
         total, slot_weights, first_moment, second_moment, left_stats, right_stats, left_basis, right_basis,
-        vector_values, vector_first, vector_second,
-    )
-    vectors = [value.reshape(-1) for value in updated[6:]]
-    return (block_out, input_half.astype(jnp.float32), *updated[:6], *vectors)
+        vector_values, vector_first, vector_second, block_land, input_land,
+    )
+    vectors = [value.reshape(-1) for value in updated[6:9]]
+    return (updated[9], updated[10], *updated[:6], *vectors)
 
 
 def solution(mesh):

time: 252 us -> 224 us (0.89)
  Pallas kernels: 242 us -> 217 us
    pallas_call x1, Pallas kernels: 90.8 us -> 74.3 us  [reduce_all(): pl.pallas_call(reduce_kernel, name='reduce_all', out_shape=[jax.ShapeDtyp...]
    pallas_call x1, Pallas kernels: 66.2 us -> 56.9 us  [run_layer(): pl.pallas_call(layer_kernel, name='run_layer', out_shape=[jax.ShapeDtypeS...]
where the time goes in v3:
time: 224 us
  Pallas kernels  217 us (97%)
  local copies, waits for them, and re-layouts  4.73 us (2%)
    pallas_call x1, Pallas kernels, reduce_all(): pl.pallas_call(reduce_kernel, name='reduce_all', out_shape=[jax.ShapeDtyp...  74.3 us
    pallas_call x1, Pallas kernels, gather_all(): pl.pallas_call(gather_kernel, name='gather_all', out_shape=[pltpu.HBM((48...  70.8 us
    pallas_call x1, Pallas kernels, run_layer(): pl.pallas_call(layer_kernel, name='run_layer', out_shape=[jax.ShapeDtypeS...  56.9 us
    pallas_call x1, Pallas kernels, update_all(): pl.pallas_call(update_kernel, name='update_all', out_shape=[matrix] * 5 +...  14.6 us

profile of v3, /device:TPU:1, one launch (start us, length us, event | category | flops | bytes accessed | tf_op | source)
XLA Modules:
  0.0 223.9 jit_solution(14312957300036511306)
XLA Ops:
  0.6 0.7 reshape.53.vector.vec
  1.3 70.8 %gather_all.1 = (bf16[48,400,384]{2,1,0:T(8,128)(2,1)}, bf16[4,128,768]{2,1,0:T(8,128)(2,1)}, bf16[4,128,768]{2,1,0:T(8,128)(2,1)}) custom-call(f32[6,384,384]{2,1,0:T(8,128)} %weights.3, f32[1,384]{1,0:T(1,128)S(1)} %reshape.53.vector.vec, bf16[4,128,768]{2,1,0:T(8,128)(2,1)} %tokens.1, bf16[4,128,768]{2,1,0:T(8,128)(2,1)} %grads.1), custom_call_target="tpu_custom_call" | custom-call | tf_op jit(solution)/shard_map/gather_all/pallas_call | solution.py:526
  72.1 56.9 %run_layer.1 = (bf16[48,400,384]{2,1,0:T(8,128)(2,1)}, bf16[512,768]{1,0:T(8,128)(2,1)}, bf16[512,768]{1,0:T(8,128)(2,1)}) custom-call(s32[48]{0:T(128)} %owner.1, bf16[48,400,384]{2,1,0:T(8,128)(2,1)} %get-tuple-element.31.weights, bf16[512,768]{1,0:T(8,128)(2,1)} %bitcast.6, bf16[512,768]{1,0:T(8,128)(2,1)} %bitcast.7, s32[4,512]{1,0:T(4,128)} %segments.1), custom_call_target="tpu_custom_call" | custom-call | tf_op jit(solution)/shard_map/run_layer/pallas_call | solution.py:855
  129.0 0.0 copy-start.6
  129.0 0.0 copy-start.7
  129.0 0.0 copy-start
  129.1 0.0 copy-start.1
  129.1 0.0 copy-start.2
  129.1 0.0 copy-start.3
  129.1 74.3 %reduce_all.1 = (bf16[6,400,384]{2,1,0:T(8,128)(2,1)S(1)}, bf16[4,128,768]{2,1,0:T(8,128)(2,1)}, bf16[4,128,768]{2,1,0:T(8,128)(2,1)}) custom-call(bf16[48,400,384]{2,1,0:T(8,128)(2,1)} %get-tuple-element.34.grads, bf16[4,128,768]{2,1,0:T(8,128)(2,1)} %bitcast.4, bf16[4,128,768]{2,1,0:T(8,128)(2,1)} %bitcast.5), custom_call_target="tpu_custom_call" | custom-call | tf_op jit(solution)/shard_map/reduce_all/pallas_call | solution.py:1162
  203.4 0.0 copy-done.6
  203.4 0.0 copy-done.7
  203.5 0.0 copy-done
  203.5 0.0 copy-done.1
  203.5 0.0 copy-done.2
  203.5 0.0 copy-done.3
  203.5 0.0 copy-start.4
  203.5 2.0 copy-done.4
  205.5 0.0 copy-start.5
  205.5 2.0 copy-done.5
  207.5 14.6 %update_all.1 = (f32[6,384,384]{2,1,0:T(8,128)}, f32[6,384,384]{2,1,0:T(8,128)}, f32[6,384,384]{2,1,0:T(8,128)}, f32[6,384,384]{2,1,0:T(8,128)}, f32[6,384,384]{...) custom-call(bf16[6,400,384]{2,1,0:T(8,128)(2,1)S(1)} %get-tuple-elem, ...), custom_call_target="tpu_custom_call" | custom-call | tf_op jit(solution)/shard_map/update_all/pallas_call | solution.py:1272
  222.1 0.6 reduce
  222.7 0.6 reduce.1
  223.3 0.6 reduce.2
  (2 shorter events, 0.0 us)
Async XLA Ops:
  129.0 74.4 %copy-start.6 = (f32[384]{0:T(512)S(1)}, f32[384]{0:T(512)}, u32[]{:S(2)}) copy-start(f32[384]{0:T(512)} %param.27) | copy-start | bytes 4612
  129.0 74.4 %copy-start.7 = (f32[384]{0:T(512)S(1)}, f32[384]{0:T(512)}, u32[]{:S(2)}) copy-start(f32[384]{0:T(512)} %param.28) | copy-start | bytes 4612
  129.0 74.4 %copy-start = (f32[6,384,384]{2,1,0:T(8,128)S(1)}, f32[6,384,384]{2,1,0:T(8,128)}, u32[]{:S(2)}) copy-start(f32[6,384,384]{2,1,0:T(8,128)} %weights.3) | copy-start | bytes 10616836
  129.1 74.4 %copy-start.1 = (f32[6,384,384]{2,1,0:T(8,128)S(1)}, f32[6,384,384]{2,1,0:T(8,128)}, u32[]{:S(2)}) copy-start(f32[6,384,384]{2,1,0:T(8,128)} %first.1) | copy-start | bytes 10616836
  129.1 74.4 %copy-start.2 = (f32[6,384,384]{2,1,0:T(8,128)S(1)}, f32[6,384,384]{2,1,0:T(8,128)}, u32[]{:S(2)}) copy-start(f32[6,384,384]{2,1,0:T(8,128)} %second.1) | copy-start | bytes 10616836
  129.1 74.4 %copy-start.3 = (f32[6,384,384]{2,1,0:T(8,128)S(1)}, f32[6,384,384]{2,1,0:T(8,128)}, u32[]{:S(2)}) copy-start(f32[6,384,384]{2,1,0:T(8,128)} %left.1) | copy-start | bytes 10616836
  203.5 2.0 copy-start.4
  205.5 2.0 copy-start.5

commit v4 on v3

--- a/solution.py
+++ b/solution.py
@@ -340,16 +340,64 @@
     pl.semaphore_wait(barrier, 4 + (z < NZ - 1).astype(jnp.int32) + (z > 0).astype(jnp.int32))
 
 
-def gather_kernel(
-    weights, vector, tokens, grads, out, token_row, grad_row,
-    wide, narrow, load_sem, keep_sem, send_sem, recv_sem, row_send, row_recv, row_keep,
-):
+PIECES = {
+    "A0": (BLK + 16, False, True),
+    "A1": (BLK // 2, False, False),
+    "O0": (BLK // 2, True, True),
+    "O1": (BLK // 4, True, True),
+}
+STEPS = (
+    ("own", "O1"), ("rows", 1), ("own", "O0"), ("own", "A1"), ("z", "O1", 1, 1, 0), ("z", "O1", 1, -1, 0),
+    ("y", "O1", 0, 0), ("z", "O0", 1, 1, 0), ("own", "A0"), ("z", "O0", 2, 1, 0), ("y", "O0", 0, 0),
+    ("z", "O0", 1, -1, 0), ("z", "O1", 2, -1, 0), ("y", "O1", 1, -1), ("z", "O1", 3, -1, 0), ("z", "A1", 1, 1, 0),
+    ("z", "O1", 2, 1, 0), ("y", "O1", 1, 1), ("z", "O0", 3, 1, 0), ("z", "A0", 1, -1, 0), ("y", "O1", 2, -1),
+    ("y", "O0", 1, 1), ("z", "O1", 3, 1, 0), ("y", "O0", 2, 1), ("x", "O0", 3, 1, 0), ("x", "O1", 3, -1, 0),
+    ("x", "O1", 1, 1, 0), ("z", "A1", 1, -1, 0), ("x", "O0", 1, -1, 0), ("z", "A0", 1, 1, 0),
+    ("x", "O1", 1, -1, 1), ("y", "O1", 3, -1), ("y", "A1", 0, 0), ("z", "A0", 2, 1, 0), ("x", "O0", 2, 1, 0),
+    ("y", "O1", 2, 1), ("rows", 0), ("z", "O0", 2, -1, 0), ("x", "O0", 2, 1, 1), ("z", "A0", 2, -1, 0),
+    ("x", "O1", 0, 0, 1), ("z", "A1", 1, 1, 1), ("x", "O0", 1, 1, 1), ("z", "O0", 3, -1, 0), ("z", "A1", 1, -1, 1),
+    ("y", "O0", 2, -1), ("y", "O0", 3, 1), ("y", "A0", 1, -1), ("x", "O1", 2, 1, 1), ("x", "O1", 3, 1, 0),
+    ("x", "O0", 0, 0, 1), ("y", "O0", 3, -1), ("z", "A0", 3, 1, 0), ("y", "O1", 3, 1), ("z", "A0", 3, -1, 0),
+    ("x", "O0", 1, 1, 0), ("x", "O1", 3, -1, 1), ("y", "O0", 1, -1), ("z", "A1", 2, -1, 0), ("y", "A0", 0, 0),
+    ("x", "O1", 2, -1, 1), ("y", "A0", 2, -1), ("z", "A1", 2, -1, 1), ("x", "O0", 2, -1, 0), ("z", "A1", 3, -1, 0),
+    ("x", "O0", 3, -1, 0), ("x", "O0", 3, -1, 1), ("z", "A1", 2, 1, 1), ("y", "A0", 2, 1), ("z", "A1", 2, 1, 0),
+    ("x", "O0", 3, 1, 1), ("x", "O1", 2, -1, 0), ("z", "A1", 3, 1, 1), ("x", "O1", 2, 1, 0), ("x", "O0", 2, -1, 1),
+    ("y", "A0", 3, -1), ("y", "A0", 1, 1), ("y", "A0", 3, 1), ("x", "O1", 3, 1, 1), ("x", "O1", 1, -1, 0),
+    ("x", "O1", 1, 1, 1), ("x", "O0", 1, -1, 1), ("z", "A1", 3, -1, 1), ("z", "A1", 3, 1, 0),
+)
+
+
+def piece_view(ref, name, x_of, c_of, base):
+    height = PIECES[name][0]
+    if name == "A0":
+        return ref.at[base + c_of, pl.ds(0, height)]
+    if name == "A1":
+        slot, row = base + 2, height * c_of
+    elif name == "O0":
+        slot, row = base + 4 + x_of, height * c_of
+    else:
+        slot, row = base + 3, 2 * height * x_of + height * c_of
+    return ref.at[slot, pl.ds(pl.multiple_of(row, height), height)]
+
+
+def gather_kernel(weights, vector, tokens, grads, out, token_row, grad_row, wide, narrow, *sems):
     z, y, x, c = place()
     dp = z * 2 + y
     sp = x * 2 + c
-    loads = [pltpu.make_async_copy(weights.at[i], wide.at[i], load_sem.at[i]) for i in range(6)]
-    for load in loads:
-        load.start()
+    sems = list(sems)
+    load_sem, keep_sem, row_send, row_recv, row_keep = [sems.pop(0) for _ in range(5)]
+    ways = ("up", "down", "y", "mate", "x", "pass")
+    send_sem = {(way, name): sems.pop(0) for way in ways for name in PIECES if PIECES[name][1] or way not in ways[4:]}
+    recv_sem = {(way, name): sems.pop(0) for way in ways[2:] for name in PIECES if PIECES[name][1] or way not in ways[4:]}
+    targets = {
+        "up": (dp + 2, sp), "down": (dp - 2, sp), "y": (z * 2 + 1 - y, sp),
+        "x": (dp, (1 - x) * 2 + c), "mate": (dp, x * 2 + 1 - c), "pass": (dp, x * 2 + 1 - c),
+    }
+    def load_of(i):
+        return pltpu.make_async_copy(weights.at[i], wide.at[i], load_sem.at[i])
+
+    for i in (c, 2, 3, 4 + x, 1 - c, 5 - x):
+        load_of(i).start()
     keeps = [
         pltpu.make_async_copy(tokens.at[sp], token_row.at[sp], row_keep.at[0]),
         pltpu.make_async_copy(grads.at[sp], grad_row.at[sp], row_keep.at[1]),
@@ -359,159 +407,106 @@
     gains = jnp.broadcast_to(vector[...], (16, BLK)).astype(jnp.bfloat16)
     greet(z, y, x, c)
 
-    def rows_copy(which, source, landing, step):
+    def row_copy(which, source, landing, step, arrival):
         peer = (sp + step) % 4
+        at = peer if arrival else sp
         return pltpu.make_async_remote_copy(
-            src_ref=source.at[peer], dst_ref=landing.at[sp],
-            send_sem=row_send.at[which, step - 1], recv_sem=row_recv.at[which, sp],
+            src_ref=source.at[peer], dst_ref=landing.at[at],
+            send_sem=row_send.at[which, step - 1], recv_sem=row_recv.at[which, at],
             device_id=(dp, peer), device_id_type=MESH,
         )
 
-    def rows_arrival(which, source, landing, step):
-        peer = (sp + step) % 4
-        return pltpu.make_async_remote_copy(
-            src_ref=source.at[peer], dst_ref=landing.at[peer],
-            send_sem=row_send.at[which, step - 1], recv_sem=row_recv.at[which, peer],
-            device_id=(dp, peer), device_id_type=MESH,
-        )
-
-    for step in (2, 3, 1):
-        rows_copy(0, tokens, token_row, step).start()
-
-    for i in range(6):
-        loads[i].wait()
+    def round_block(i):
+        load_of(i).wait()
         narrow[i, :BLK, :] = wide[i].astype(jnp.bfloat16)
         narrow[i, BLK:, :] = gains
+
+    for i in (c, 2, 3, 4 + x):
+        round_block(i)
     own = [pltpu.make_async_copy(narrow.at[i], out.at[dp * 6 + i], keep_sem.at[i]) for i in range(6)]
-
-    def piece(part):
-        return (c, BLK + 16) if part == 0 else (2 + 2 * x + c, BLK)
-
-    targets = {
-        "up": (dp + 2, sp), "down": (dp - 2, sp), "y": (z * 2 + 1 - y, sp),
-        "x": (dp, (1 - x) * 2 + c), "core": (dp, x * 2 + 1 - c),
-    }
-    number = {"up": 0, "down": 1, "y": 2, "x": 3, "core": 4}
-
-    def copy(way, holder, slot, height, index, source=None):
-        at = holder * 6 + slot
-        src = out.at[at, pl.ds(0, height)] if source is None else source
+    started = []
+
+    def item_of(way, name, holder, x_of, c_of, fresh=False):
+        landing = piece_view(out, name, x_of, c_of, holder * 6)
+        arrives = way if way in ("mate", "x", "pass") else "y"
         return pltpu.make_async_remote_copy(
-            src_ref=src, dst_ref=out.at[at, pl.ds(0, height)],
-            send_sem=send_sem.at[number[way], index], recv_sem=recv_sem.at[at],
+            src_ref=piece_view(narrow, name, x_of, c_of, 0) if fresh else landing, dst_ref=landing,
+            send_sem=send_sem[way, name].at[holder], recv_sem=recv_sem[arrives, name].at[holder],
             device_id=targets[way], device_id_type=MESH,
         )
 
-    started = []
-
-    def start(way, holder, slot, height, index, valid=None, source=None):
-        item = copy(way, holder, slot, height, index, source)
+    def send(way, name, holder, valid, x_of=x, fresh=False):
+        if way in ("up", "down"):
+            room = z < NZ - 1 if way == "up" else z > 0
+            valid = room if valid is None else valid & room
+        item = item_of(way, name, holder, x_of, c, fresh)
         if valid is None:
             item.start()
         else:
             pl.when(valid)(item.start)
         started.append((item, valid))
 
-    def arrive(holder, slot, height, valid=None):
-        item = copy("core", holder, slot, height, 0)
+    def arrive(way, name, holder, valid, x_of, c_of):
+        item = item_of(way, name, holder, x_of, c_of)
         if valid is None:
             item.wait_recv()
         else:
             pl.when(valid)(item.wait_recv)
 
-    counts = {}
-
-    def fresh(way):
-        counts[way] = counts.get(way, -1) + 1
-        return counts[way]
-
-    for part in (1, 0):
-        slot, height = piece(part)
-        src = narrow.at[slot, pl.ds(0, height)]
-        start("up", dp, slot, height, fresh("up"), z < NZ - 1, src)
-        start("down", dp, slot, height, fresh("down"), z > 0, src)
-        start("y", dp, slot, height, fresh("y"), None, src)
-    for item in own:
-        item.start()
-
-    def from_z(sign, far, part):
-        origin = z + sign * far
-        inside = (origin >= 0) if sign < 0 else (origin <= NZ - 1)
-        holder = origin * 2 + y
-        slot, height = piece(part)
-        arrive(holder, slot, height, inside)
-        if far < NZ - 1:
-            if sign < 0:
-                start("up", holder, slot, height, fresh("up"), inside & (z < NZ - 1))
-            else:
-                start("down", holder, slot, height, fresh("down"), inside & (z > 0))
-        start("y", holder, slot, height, fresh("y"), inside)
-        if part == 1:
-            start("x", holder, slot, height, fresh("x"), inside)
-        start("core", holder, slot, height, fresh("core"), inside)
-
-    def signs(far):
-        return (0,) if far == 0 else (-1, 1)
-
-    def valid_of(sign, far):
+    def origin_of(sign, far):
         origin = z + sign * far
         if far == 0:
             return origin, None
         return origin, ((origin >= 0) if sign < 0 else (origin <= NZ - 1))
 
-    def from_y(sign, far, part):
-        origin, inside = valid_of(sign, far)
-        holder = origin * 2 + 1 - y
-        slot, height = piece(part)
-        arrive(holder, slot, height, inside)
-        if part == 1:
-            start("x", holder, slot, height, fresh("x"), inside)
-        start("core", holder, slot, height, fresh("core"), inside)
-
-    def from_x(sign, far, side):
-        origin, inside = valid_of(sign, far)
-        holder = origin * 2 + (y if side == 0 else 1 - y)
-        slot = 2 + 2 * (1 - x) + c
-        arrive(holder, slot, BLK, inside)
-        start("core", holder, slot, BLK, fresh("core"), inside)
-
-    for far in range(1, NZ):
-        for part in (1, 0):
-            for sign in (-1, 1):
-                from_z(sign, far, part)
-            for sign in signs(far - 1):
-                from_y(sign, far - 1, part)
-        if far == 1:
-            for step in (2, 3, 1):
-                rows_copy(1, grads, grad_row, step).start()
-        if far >= 2:
-            for sign in signs(far - 1):
-                from_x(sign, far - 1, 0)
-            for sign in signs(far - 2):
-                from_x(sign, far - 2, 1)
-    for part in (1, 0):
-        for sign in (-1, 1):
-            from_y(sign, NZ - 1, part)
-    for sign in (-1, 1):
-        from_x(sign, NZ - 1, 0)
-    for far in (NZ - 2, NZ - 1):
-        for sign in signs(far):
-            from_x(sign, far, 1)
+    for step in STEPS:
+        kind, name = step[0], step[1]
+        if kind == "own":
+            for way in ("up", "down", "y"):
+                send(way, name, dp, None, fresh=True)
+        elif kind == "rows":
+            source, landing = ((tokens, token_row), (grads, grad_row))[name]
+            for hop in (2, 3, 1):
+                row_copy(name, source, landing, hop, False).start()
+        else:
+            origin, inside = origin_of(step[3], step[2])
+            if kind == "x":
+                holder = origin * 2 + (y if step[4] == 0 else 1 - y)
+                arrive("x", name, holder, inside, 1 - x, c)
+                send("pass", name, holder, inside, 1 - x)
+                continue
+            holder = origin * 2 + (y if kind == "z" and step[4] == 0 else 1 - y)
+            arrive("y", name, holder, inside, x, c)
+            if kind == "z":
+                if step[2] < NZ - 1:
+                    send("up" if step[3] < 0 else "down", name, holder, inside)
+                if PIECES[name][2] and step[4] == 0:
+                    send("y", name, holder, inside)
+            elif not PIECES[name][2]:
+                send("up", name, holder, inside)
+                send("down", name, holder, inside)
+            if PIECES[name][1]:
+                send("x", name, holder, inside)
+            send("mate", name, holder, inside)
+        if kind == "own" and name == "A0":
+            for i in (1 - c, 5 - x):
+                round_block(i)
+            for item in own:
+                item.start()
 
     for far in range(NZ):
-        for sign in signs(far):
-            origin, inside = valid_of(sign, far)
-            for side in (0, 1):
-                if far == 0 and side == 0:
-                    continue
-                holder = origin * 2 + (y if side == 0 else 1 - y)
-                for slot, height in ((1 - c, BLK + 16), (3 - c, BLK), (5 - c, BLK)):
-                    arrive(holder, slot, height, inside)
-    for step in (2, 3, 1):
-        rows_arrival(0, tokens, token_row, step).wait_recv()
-        rows_arrival(1, grads, grad_row, step).wait_recv()
-        rows_copy(0, tokens, token_row, step).wait_send()
-        rows_copy(1, grads, grad_row, step).wait_send()
+        for sign in (0,) if far == 0 else (-1, 1):
+            origin, inside = origin_of(sign, far)
+            for column in (1,) if far == 0 else (0, 1):
+                holder = origin * 2 + (y if column == 0 else 1 - y)
+                for name in PIECES:
+                    arrive("mate", name, holder, inside, x, 1 - c)
+                    if PIECES[name][1]:
+                        arrive("pass", name, holder, inside, 1 - x, 1 - c)
+    for hop in (2, 3, 1):
+        for which, source, landing in ((0, tokens, token_row), (1, grads, grad_row)):
+            row_copy(which, source, landing, hop, True).wait_recv()
+            row_copy(which, source, landing, hop, False).wait_send()
     for item, valid in started:
         if valid is None:
             item.wait_send()
@@ -522,7 +517,10 @@
 
 
 def gather_all(weights, vector, tokens, grads):
-    anywhere = pl.BlockSpec(memory_space=pltpu.HBM)
+    anywhere = pl.BlockSpec(memory_space=pl.ANY)
+    dma = pltpu.SemaphoreType.DMA
+    carried = sum(1 for name in PIECES if PIECES[name][1])
+    flows = (4 * len(PIECES) + 2 * carried) + (2 * len(PIECES) + 2 * carried)
     return pl.pallas_call(
         gather_kernel,
         name="gather_all",
@@ -536,14 +534,9 @@
         scratch_shapes=[
             pltpu.VMEM((6, BLK, BLK), jnp.float32),
             pltpu.VMEM((6, PITCH, BLK), jnp.bfloat16),
-            pltpu.SemaphoreType.DMA((6,)),
-            pltpu.SemaphoreType.DMA((6,)),
-            pltpu.SemaphoreType.DMA((5, 40)),
-            pltpu.SemaphoreType.DMA((48,)),
-            pltpu.SemaphoreType.DMA((2, 3)),
-            pltpu.SemaphoreType.DMA((2, 4)),
-            pltpu.SemaphoreType.DMA((2,)),
-        ],
+            dma((6,)), dma((6,)), dma((2, 3)), dma((2, 4)), dma((2,)),
+        ]
+        + [dma((8,))] * flows,
         compiler_params=pltpu.CompilerParams(
             collective_id=0, has_side_effects=True, vmem_limit_bytes=24 << 20
         ),
@@ -678,7 +671,7 @@
     acc[...] = dot_nn(joined, wo[...])
 
     def norm_one(t, carry):
-        rows = pl.ds(pl.multiple_of(t * 64, 64), 64)
+        rows = pl.ds(pl.multiple_of(t * 128, 128), 128)
         hat, inverse = normalise(tokens[rows, :].astype(jnp.float32) + acc[rows, :])
         norm1[rows, :] = hat
         spread[rows, :] = jnp.where(lane == 1, inverse, spread[rows, :])
@@ -687,7 +680,7 @@
         hidden16[rows, :] = value.astype(half)
         return carry
 
-    lax.fori_loop(0, 8, norm_one, 0)
+    lax.fori_loop(0, 4, norm_one, 0)
     for item in copies[16:]:
         item.wait()
 
@@ -713,7 +706,7 @@
         ) * inverse
 
     def norm_two(t, carry):
-        rows = pl.ds(pl.multiple_of(t * 64, 64), 64)
+        rows = pl.ds(pl.multiple_of(t * 128, 128), 128)
         hat, inverse = normalise(hidden[rows, :])
         block_out[rows, :] = (hat * gain(2) + gain(3)).astype(half)
         delta = dy_ref[rows, :].astype(jnp.float32)
@@ -724,7 +717,7 @@
         dz16[rows, :] = back.astype(half)
         return carry
 
-    lax.fori_loop(0, 8, norm_two, 0)
+    lax.fori_loop(0, 4, norm_two, 0)
 
     def out_copy(slot, b, r, q):
         return pltpu.make_async_copy(
@@ -762,7 +755,7 @@
     lax.fori_loop(0, 4, backward, 0)
 
     def norm_one_back(t, carry):
-        rows = pl.ds(pl.multiple_of(t * 64, 64), 64)
+        rows = pl.ds(pl.multiple_of(t * 128, 128), 128)
         hat = norm1[rows, :]
         delta = dz[rows, :]
         vecs[0] += fold(delta * hat)
@@ -772,7 +765,7 @@
         dz16[rows, :] = back.astype(half)
         return carry
 
-    lax.fori_loop(0, 8, norm_one_back, 0)
+    lax.fori_loop(0, 4, norm_one_back, 0)
 
     for slot in range(4):
         drain(slot)
@@ -1193,15 +1186,26 @@
 
 
 def update_kernel(
-    total, weights, first, second, left, right, left_rot, right_rot, vec, vec_first, vec_second, land_a, land_b,
-    moment_one, moment_two, left_new, right_new, weights_new, weights_half, vector_one, vector_two, vector_new,
-    rows_a, rows_b, held, narrow, wide, stage, stage_half, out_sem, sems,
+    total, weights, first, second, left_old, right_old, left_rot, right_rot, vec, vec_first, vec_second, land_a,
+    land_b, moment_one, moment_two, left_new, right_new, weights_new, weights_half, vector_one, vector_two, vector_new,
+    rows_a, rows_b, held, narrow, wide, stage, stage_half, left, right, out_sem, in_sem, sems,
 ):
     half = jnp.bfloat16
     take_a = pltpu.make_async_copy(land_a, held, sems.at[0])
     give_a = pltpu.make_async_copy(held, rows_a, sems.at[3])
     take_b = pltpu.make_async_copy(land_b, narrow, sems.at[1])
     give_b = pltpu.make_async_copy(wide, rows_b, sems.at[2])
+    count = weights.shape[0]
+
+    def state_of(i):
+        return [
+            pltpu.make_async_copy(old.at[i], now.at[i], in_sem.at[i, k])
+            for k, (old, now) in enumerate(((left_old, left), (right_old, right)))
+        ]
+
+    for i in range(count):
+        for item in state_of(i):
+            item.start()
     take_b.start()
     take_a.start()
     slope = total[0, pl.ds(BLK, 1), :].astype(jnp.float32)
@@ -1222,6 +1226,9 @@
         return copies + [pltpu.make_async_copy(stage_half.at[i], weights_half.at[i], out_sem.at[i, 5])]
 
     def blocks(pair, carry):
+        for i in [pair * GROUP + k for k in range(GROUP)]:
+            for item in state_of(i):
+                item.wait()
         for i in [pair * GROUP + k for k in range(GROUP)]:
             grad = total[i, :BLK, :]
             rot_l = left_rot[i].astype(half)
@@ -1274,7 +1281,7 @@
         name="update_all",
         out_shape=[matrix] * 5 + [pltpu.HBM(weights.shape, jnp.bfloat16)] + [vector] * 3
         + [pltpu.HBM(land_a.shape, jnp.bfloat16), pltpu.HBM(land_b.shape, full)],
-        in_specs=[vmem] * 11 + [anywhere] * 2,
+        in_specs=[vmem] * 4 + [anywhere] * 2 + [vmem] * 5 + [anywhere] * 2,
         out_specs=[anywhere] * 6 + [vmem] * 3 + [anywhere] * 2,
         scratch_shapes=[
             pltpu.VMEM(land_a.shape, jnp.bfloat16),
@@ -1282,12 +1289,15 @@
             pltpu.VMEM(land_b.shape, full),
             pltpu.VMEM((5, *weights.shape), full),
             pltpu.VMEM(weights.shape, jnp.bfloat16),
+            pltpu.VMEM(weights.shape, full),
+            pltpu.VMEM(weights.shape, full),
             pltpu.SemaphoreType.DMA((weights.shape[0], 6)),
+            pltpu.SemaphoreType.DMA((weights.shape[0], 2)),
             pltpu.SemaphoreType.DMA((4,)),
         ],
-        compiler_params=pltpu.CompilerParams(vmem_limit_bytes=30 << 20),
+        compiler_params=pltpu.CompilerParams(vmem_limit_bytes=38 << 20),
     )(
-        total, weights, first, second, left, right, left_rot, right_rot,
+        total, weights, first, second, in_hbm(left), in_hbm(right), left_rot, right_rot,
         vec.reshape(1, BLK), vec_first.reshape(1, BLK), vec_second.reshape(1, BLK), in_hbm(land_a), in_hbm(land_b),
     )
 

time: 224 us -> 212 us (0.946)
  Pallas kernels: 217 us -> 208 us
  local copies, waits for them, and re-layouts: 4.73 us -> 0.73 us
    pallas_call x1, Pallas kernels: 70.8 us -> 63.6 us  [gather_all(): pl.pallas_call(gather_kernel, name='gather_all', out_shape=[pltpu.HBM((48...]
    unnamed x16 -> x12, local copies, waits for them, and re-layouts: 4.03 us -> 0.04 us
where the time goes in v4:
time: 212 us; the launch traced here: 211 us
  Pallas kernels  208 us (98%)
    pallas_call x1, Pallas kernels, reduce_all(): pl.pallas_call(reduce_kernel, name='reduce_all', out_shape=[jax.ShapeDtyp...  73.4 us
    pallas_call x1, Pallas kernels, gather_all(): pl.pallas_call(gather_kernel, name='gather_all', out_shape=[pltpu.HBM((48...  63.6 us
    pallas_call x1, Pallas kernels, run_layer(): pl.pallas_call(layer_kernel, name='run_layer', out_shape=[jax.ShapeDtypeS...  54.9 us
    pallas_call x1, Pallas kernels, update_all(): pl.pallas_call(update_kernel, name='update_all', out_shape=[matrix] * 5 +...  16.2 us

profile of v4, /device:TPU:1, one launch (start us, length us, event | category | flops | bytes accessed | tf_op | source)
XLA Modules:
  0.0 211.4 jit_solution(568092384320575564)
XLA Ops:
  0.6 0.7 reshape.53.vector.vec
  1.3 63.6 %gather_all.1 = (bf16[48,400,384]{2,1,0:T(8,128)(2,1)}, bf16[4,128,768]{2,1,0:T(8,128)(2,1)}, bf16[4,128,768]{2,1,0:T(8,128)(2,1)}) custom-call(f32[6,384,384]{2,1,0:T(8,128)} %weights.3, f32[1,384]{1,0:T(1,128)S(1)} %reshape.53.vector.vec, bf16[4,128,768]{2,1,0:T(8,128)(2,1)} %tokens.1, bf16[4,128,768]{2,1,0:T(8,128)(2,1)} %grads.1), custom_call_target="tpu_custom_call" | custom-call | tf_op jit(solution)/shard_map/gather_all/pallas_call | solution.py:524
  64.9 54.9 %run_layer.1 = (bf16[48,400,384]{2,1,0:T(8,128)(2,1)}, bf16[512,768]{1,0:T(8,128)(2,1)}, bf16[512,768]{1,0:T(8,128)(2,1)}) custom-call(s32[48]{0:T(128)} %owner.1, bf16[48,400,384]{2,1,0:T(8,128)(2,1)} %get-tuple-element.31.weights, bf16[512,768]{1,0:T(8,128)(2,1)} %bitcast.6, bf16[512,768]{1,0:T(8,128)(2,1)} %bitcast.7, s32[4,512]{1,0:T(4,128)} %segments.1), custom_call_target="tpu_custom_call" | custom-call | tf_op jit(solution)/shard_map/run_layer/pallas_call | solution.py:848
  119.8 0.0 copy-start.4
  119.8 0.0 copy-start.5
  119.9 0.0 copy-start
  119.9 0.0 copy-start.1
  119.9 0.0 copy-start.2
  119.9 0.0 copy-start.3
  119.9 73.4 %reduce_all.1 = (bf16[6,400,384]{2,1,0:T(8,128)(2,1)S(1)}, bf16[4,128,768]{2,1,0:T(8,128)(2,1)}, bf16[4,128,768]{2,1,0:T(8,128)(2,1)}) custom-call(bf16[48,400,384]{2,1,0:T(8,128)(2,1)} %get-tuple-element.34.grads, bf16[4,128,768]{2,1,0:T(8,128)(2,1)} %bitcast.4, bf16[4,128,768]{2,1,0:T(8,128)(2,1)} %bitcast.5), custom_call_target="tpu_custom_call" | custom-call | tf_op jit(solution)/shard_map/reduce_all/pallas_call | solution.py:1155
  193.3 0.0 copy-done.4
  193.3 0.0 copy-done.5
  193.3 0.0 copy-done
  193.3 0.0 copy-done.1
  193.3 0.0 copy-done.2
  193.4 0.0 copy-done.3
  193.4 16.2 %update_all.1 = (f32[6,384,384]{2,1,0:T(8,128)}, f32[6,384,384]{2,1,0:T(8,128)}, f32[6,384,384]{2,1,0:T(8,128)}, f32[6,384,384]{2,1,0:T(8,128)}, f32[6,384,384]{...) custom-call(bf16[6,400,384]{2,1,0:T(8,128)(2,1)S(1)} %get-tuple-elem, ...), custom_call_target="tpu_custom_call" | custom-call | tf_op jit(solution)/shard_map/update_all/pallas_call | solution.py:1279
  209.6 0.6 reduce
  210.2 0.6 reduce.1
  210.8 0.6 reduce.2
  (2 shorter events, 0.0 us)
Async XLA Ops:
  119.8 73.5 %copy-start.4 = (f32[384]{0:T(512)S(1)}, f32[384]{0:T(512)}, u32[]{:S(2)}) copy-start(f32[384]{0:T(512)} %param.27) | copy-start | bytes 4612
  119.8 73.5 %copy-start.5 = (f32[384]{0:T(512)S(1)}, f32[384]{0:T(512)}, u32[]{:S(2)}) copy-start(f32[384]{0:T(512)} %param.28) | copy-start | bytes 4612
  119.9 73.5 %copy-start = (f32[6,384,384]{2,1,0:T(8,128)S(1)}, f32[6,384,384]{2,1,0:T(8,128)}, u32[]{:S(2)}) copy-start(f32[6,384,384]{2,1,0:T(8,128)} %weights.3) | copy-start | bytes 10616836
  119.9 73.5 %copy-start.1 = (f32[6,384,384]{2,1,0:T(8,128)S(1)}, f32[6,384,384]{2,1,0:T(8,128)}, u32[]{:S(2)}) copy-start(f32[6,384,384]{2,1,0:T(8,128)} %first.1) | copy-start | bytes 10616836
  119.9 73.5 %copy-start.2 = (f32[6,384,384]{2,1,0:T(8,128)S(1)}, f32[6,384,384]{2,1,0:T(8,128)}, u32[]{:S(2)}) copy-start(f32[6,384,384]{2,1,0:T(8,128)} %second.1) | copy-start | bytes 10616836
  119.9 73.5 %copy-start.3 = (f32[6,384,384]{2,1,0:T(8,128)S(1)}, f32[6,384,384]{2,1,0:T(8,128)}, u32[]{:S(2)}) copy-start(f32[6,384,384]{2,1,0:T(8,128)} %left_rot.1) | copy-start | bytes 10616836
